TPU v7x, 32 devices: a whole 2x2x4 slice. The times are simulated.
32 devices in a mesh: row: 2 (over core), blk: 16 (over z, y, x).
Axes of the slice: x: 2, y: 2, z: 4, core: 2. Of those that a mesh axis runs over, the one named last changes fastest.
Arguments:
- state: float32 [2, 5, 512, 512], P('row', None, 'blk'), may hold values from -6 to 6
- forcing: float32 [2, 5, 512, 512], P('row', None, 'blk'), may hold values from -6 to 6
- sigma: float32 [2, 512, 512], P('row', 'blk'), may hold values from 0.05 to 2
- partner: int32 [2, 512, 1], P('row', 'blk'), may hold values from 0 to 15; in each aligned block of 32 rows (0 to 31, 32 to 63, ..., all dimensions but the last counted through in order) at most 4 rows name the same one
- loop_weight: float32 [2, 128], P('row'), may hold values from 0.05 to 0.2
- offset: int32 [1], replicated, may hold values from 0 to 127
Outputs:
- solution: float32 [2, 5, 512, 512], P('row', None, 'blk')
- loop_correction: float32 [2, 5, 128], P('row', None, 'blk')
Inputs may be any that keep to these rules, and one draw needn't show every extreme that they name: Among the 32 face cells of one device no partner slot is named more than 4 times.
All inputs are finite; a program needn't handle non-finite values.
Results may differ from a plain program's by a relative error of at most 0.00011.
Values sent between devices are 32-bit elements; how exact they have to be, the bound alone decides.
No kernel may reach another device: no remote copies, remote signals or barrier semaphores. Data moves between devices by JAX's collectives and lax.ppermute only.
A program may use at most 64 MiB of HBM per device.

v0:
```python
import functools

import jax
import jax.numpy as jnp
from jax import lax
from jax.experimental import pallas as pl
from jax.experimental.pallas import tpu as pltpu
from jax.sharding import PartitionSpec as P

SECTIONS1 = 3
SECTIONS2 = 3
SECTIONS3 = 4
COEFF = 0.8

FOLD = 4


def vmem():
    return pl.BlockSpec(memory_space=pltpu.VMEM)


def lanes_of(rows, cols):
    return lax.broadcasted_iota(jnp.int32, (rows, cols), 1)


def rows_of(rows, cols):
    return lax.broadcasted_iota(jnp.int32, (rows, cols), 0)


def pick(x, index):
    return jnp.take_along_axis(x, index, axis=1, mode="promise_in_bounds")


def split_lanes(x):
    rows, cols = x.shape
    wide = cols // FOLD
    run = wide // FOLD
    lane = lanes_of(rows, wide)
    parts = [x[:, c * wide : (c + 1) * wide] for c in range(FOLD)]
    group = lane // run
    out = []
    for b in range(FOLD):
        index = (lane % run) * FOLD + b
        taken = [pick(p, index) for p in parts]
        value = taken[-1]
        for c in range(FOLD - 1):
            value = jnp.where(group == c, taken[c], value)
        out.append(value)
    return out


def join_lanes(parts):
    rows, wide = parts[0].shape
    run = wide // FOLD
    lane = lanes_of(rows, wide)
    turn = lane % FOLD
    out = []
    for c in range(FOLD):
        index = lane // FOLD + c * run
        taken = [pick(p, index) for p in parts]
        value = taken[-1]
        for b in range(FOLD - 1):
            value = jnp.where(turn == b, taken[b], value)
        out.append(value)
    return out


def residual(src, source, diag, scale, a, b, fold, rows):
    count = src.shape[0]
    total, wide = src.shape[-2:]
    u = [src[v, a, b][:rows] for v in range(count)]
    q = u[0] * u[0]
    for v in range(1, count):
        q = q + u[v] * u[v]
    q = q * (1.0 / count)
    factor = diag + 0.5 * q / (1.0 + q)
    lane = lanes_of(rows, wide)
    out = []
    for v in range(count):
        up = src[v, a - 1, b] if a else pltpu.roll(src[v, fold - 1, b], 1, 0)
        down = src[v, a + 1, b] if a < fold - 1 else pltpu.roll(src[v, 0, b], total - 1, 0)
        if b:
            left = src[v, a, b - 1][:rows]
        else:
            left = jnp.where(lane == 0, 0.0, pltpu.roll(src[v, a, fold - 1][:rows], 1, 1))
        if b < fold - 1:
            right = src[v, a, b + 1][:rows]
        else:
            right = jnp.where(lane == wide - 1, 0.0, pltpu.roll(src[v, a, 0][:rows], wide - 1, 1))
        near = (up[:rows] + down[:rows]) + (left + right)
        out.append(source[v, a, b][:rows] + scale * near - factor * u[v])
    return out


def section(dst, src, start, source, sigma, scale, weight, fold, rows):
    for a in range(fold):
        for b in range(fold):
            diag = 4.0 * scale + sigma[a, b][:rows]
            step = weight * (COEFF / (diag + 1.5))
            res = residual(src, source, diag, scale, a, b, fold, rows)
            for v, r in enumerate(res):
                dst[v, a, b, :rows] = start[v, a, b][:rows] + step * r


def first_section(dst, start, coarse, sigma, scale, weight, fold):
    for a in range(fold):
        for b in range(fold):
            step = weight * (COEFF / (4.0 * scale + sigma[a, b] + 1.5))
            for v in range(dst.shape[0]):
                dst[v, a, b] = start[v, a, b] + step * coarse[v, a, b]


def quarter(x):
    return 0.25 * ((x(0, 0) + x(0, 1)) + (x(1, 0) + x(1, 1)))


def wrap(x, size):
    return x & (size - 1) if size & (size - 1) == 0 else lax.rem(x, size)


def pack_kernel(s_head, s_tail, f_head, f_tail, g_head, g_tail, p_ref, head, tail):
    count = s_head.shape[1]
    rows = p_ref.shape[1]
    cols = head.shape[1]
    edge = FOLD
    deep = s_tail.shape[2]
    for v in range(count):
        for k, (top, bottom) in enumerate(((s_head, s_tail), (f_head, f_tail))):
            at = (k * count + v) * edge
            head[at : at + edge] = top[0, v, :edge]
            tail[at : at + edge] = bottom[0, v, deep - edge :]
    at = 2 * count * edge
    head[at : at + edge] = g_head[0, :edge]
    tail[at : at + edge] = g_tail[0, deep - edge :]
    at += edge
    head[at : at + edge] = jnp.broadcast_to(p_ref[0, :edge].astype(jnp.float32), (edge, cols))
    tail[at : at + edge] = jnp.broadcast_to(p_ref[0, rows - edge :].astype(jnp.float32), (edge, cols))


def fold_kernel(s_ref, f_ref, g_ref, st, fo, sg, stage):
    rows = st.shape[-2]
    count = st.shape[0]
    for ch in range(2 * count + 1):
        kind, v = divmod(ch, count)
        x = g_ref[0] if kind == 2 else (s_ref, f_ref)[kind][0, v]
        for b, part in enumerate(split_lanes(x)):
            stage[ch, b] = part
        for a in range(FOLD):
            for b in range(FOLD):
                part = stage[ch, b, pl.ds(a, rows, stride=FOLD), :]
                if kind == 2:
                    sg[a, b] = part
                else:
                    (st, fo)[kind][v, a, b] = part


def down_kernel(
    st, fo, sg, below, above, p_ref,
    u1, source, sigma, cells, head, tail, loop,
    start, buf_a, buf_b, edge_buf, resid, own_slot,
):
    count = st.shape[0]
    R, J = st.shape[-2:]
    N = loop.shape[1]
    edge = FOLD
    row = lax.axis_index("row")
    blk = lax.axis_index("blk")
    blocks = lax.axis_size("blk")
    sub = rows_of(R, J)
    for ch in range(2 * count + 1):
        x = jnp.concatenate(
            [below[ch * edge : (ch + 1) * edge], above[ch * edge : (ch + 1) * edge]], axis=0
        )
        for b, part in enumerate(split_lanes(x)):
            edge_buf[ch, b] = part

    def halo(ch, a, b):
        low = edge_buf[ch, b, a : a + 1]
        high = edge_buf[ch, b, edge + a : edge + a + 1]
        return jnp.where(sub == 0, high, jnp.where(sub == R - 1, low, 0.0))

    own_slot[...] = jnp.broadcast_to(p_ref[0], own_slot.shape)
    for a in range(FOLD):
        for b in range(FOLD):
            for v in range(count):
                start[v, a, b, :R] = st[v, a, b]
                start[v, a, b, R:] = halo(v, a, b)
                source[v, a, b, :R] = fo[v, a, b]
                source[v, a, b, R:] = halo(count + v, a, b)
            sigma[a, b, :R] = sg[a, b]
            sigma[a, b, R:] = halo(2 * count, a, b)
        at = (2 * count + 1) * edge + a
        own = own_slot[pl.ds(a, R, stride=FOLD), :]
        low = below[at : at + 1, :J].astype(jnp.int32)
        high = above[at : at + 1, :J].astype(jnp.int32)
        cells[a, :R] = wrap(own * blocks + blk, N)
        cells[a, R:] = jnp.where(
            sub < R // 2,
            wrap(high * blocks + lax.rem(blk + 1, blocks), N),
            wrap(low * blocks + lax.rem(blk + blocks - 1, blocks), N),
        )

    src = start
    for k in range(SECTIONS1):
        dst = (buf_a, buf_b)[k % 2]
        section(dst, src, start, source, sigma, 1.0, 1.0 / (SECTIONS1 - k), FOLD, 2 * R)
        src = dst

    for a in range(FOLD):
        for b in range(FOLD):
            res = residual(src, source, 4.0 + sigma[a, b][:R], 1.0, a, b, FOLD, R)
            for v in range(count):
                resid[v, a, b] = res[v]
                u = src[v, a, b][:R]
                u1[v, a, b] = u
                at = (v * FOLD + a) * FOLD + b
                k = (2 * count + 1) * 4 + at // R
                head[k, at % R : at % R + 1] = u[:1]
                tail[k, at % R : at % R + 1] = u[R - 1 :]
    for a in range(2):
        for b in range(2):
            for v in range(count):
                at = (v * 2 + a) * 2 + b
                x = quarter(lambda i, j: u1[v, 2 * a + i, 2 * b + j])
                head[at] = x
                tail[at] = x
                at += 4 * count
                x = quarter(lambda i, j: resid[v, 2 * a + i, 2 * b + j])
                head[at] = x
                tail[at] = x
            at = 8 * count + a * 2 + b
            x = quarter(lambda i, j: sg[2 * a + i, 2 * b + j])
            head[at] = x
            tail[at] = x

    lane = lanes_of(R, J)
    ring = lanes_of(R, N)
    sums = [jnp.zeros((R, N), jnp.float32) for _ in range(count)]
    column = jnp.where(row == 0, J - 1, 0)
    for a in range(FOLD):
        match = cells[a, :R, :1] == ring
        for v in range(count):
            face = jnp.where(row == 0, resid[v, a, FOLD - 1], resid[v, a, 0])
            face = jnp.sum(jnp.where(lane == column, face, 0.0), axis=1, keepdims=True)
            sums[v] = sums[v] + jnp.where(match, face, 0.0)
    loop[...] = jnp.zeros_like(loop)
    half = loop.shape[0] // 2
    for v in range(count):
        total = jnp.sum(sums[v], axis=0, keepdims=True)
        for r in range(2):
            at = r * half + v
            loop[at : at + 1] = jnp.where(row == r, total, 0.0)


def up_kernel(
    own, below, above, u1, source, sigma, cells, loop, weight_ref, offset_ref,
    solution_ref, loop_out,
    u2s, r2s, s2, f2, u3s, r3s, s3, f3, buf2a, buf2b, buf3a, buf3b,
    n2, nf2, ns2, nu2s, nb2, start, buf_a, buf_b, corr_ref, stage,
):
    count = u1.shape[0]
    R, J = u1.shape[-2:]
    N = loop.shape[1]
    row = lax.axis_index("row")
    blk = lax.axis_index("blk")
    sub = rows_of(R, J)

    for at in range(8 * count + 4):
        if at < 8 * count:
            kind, rest = divmod(at, 4 * count)
            v, ab = divmod(rest, 4)
            a, b = divmod(ab, 2)
            dst = (u2s, r2s)[kind].at[v, a, b]
        else:
            a, b = divmod(at - 8 * count, 2)
            dst = s2.at[a, b]
        dst[:R] = own[at]
        dst[R : 2 * R] = above[at]
        dst[2 * R :] = below[at]

    for a in range(2):
        for b in range(2):
            res = residual(u2s, r2s, 1.0 + s2[a, b], 0.25, a, b, 2, 3 * R)
            for v in range(count):
                f2[v, a, b] = 2.0 * r2s[v, a, b] - res[v]
    first_section(buf2a, u2s, r2s, s2, 0.25, 1.0 / SECTIONS2, 2)
    src, dst = buf2a, buf2b
    for k in range(1, SECTIONS2):
        section(dst, src, u2s, f2, s2, 0.25, 1.0 / (SECTIONS2 - k), 2, 3 * R)
        src, dst = dst, src
    u2, r2 = src, dst
    for a in range(2):
        for b in range(2):
            res = residual(u2, f2, 1.0 + s2[a, b], 0.25, a, b, 2, 3 * R)
            for v in range(count):
                r2[v, a, b] = res[v]
    for v in range(count):
        u3s[v, 0, 0] = quarter(lambda i, j: u2[v, i, j])
        r3s[v, 0, 0] = quarter(lambda i, j: r2[v, i, j])
    s3[0, 0] = quarter(lambda i, j: s2[i, j])

    res = residual(u3s, r3s, 0.25 + s3[0, 0], 0.0625, 0, 0, 1, 3 * R)
    for v in range(count):
        f3[v, 0, 0] = 2.0 * r3s[v, 0, 0] - res[v]
    first_section(buf3a, u3s, r3s, s3, 0.0625, 1.0 / SECTIONS3, 1)
    src3, dst3 = buf3a, buf3b
    for k in range(1, SECTIONS3):
        section(dst3, src3, u3s, f3, s3, 0.0625, 1.0 / (SECTIONS3 - k), 1, 3 * R)
        src3, dst3 = dst3, src3

    def narrow(x):
        return x[:R], jnp.where(sub < R // 2, x[R : 2 * R], x[2 * R :])

    for v in range(count):
        gain = narrow(src3[v, 0, 0] - u3s[v, 0, 0])
        for a in range(2):
            for b in range(2):
                for part in range(2):
                    at = slice(part * R, (part + 1) * R)
                    n2[v, a, b, at] = narrow(u2[v, a, b])[part] + gain[part]
                    nf2[v, a, b, at] = narrow(f2[v, a, b])[part]
                    if v == 0:
                        ns2[a, b, at] = narrow(s2[a, b])[part]
    src, other = n2, nb2
    spare = nu2s
    for k in range(SECTIONS2):
        dst = (nb2, spare)[k % 2]
        section(dst, src, n2, nf2, ns2, 0.25, 1.0 / (SECTIONS2 - k), 2, 2 * R)
        src = dst

    half = loop.shape[0] // 2
    mine = jnp.where(row == 0, loop[:half], loop[half:])
    others = jnp.where(row == 0, loop[half:], loop[:half])
    offset = offset_ref[0]
    shift = lax.rem(jnp.where(row == 0, N - offset, offset), N)
    correction = weight_ref[...] * (mine + pltpu.roll(others, shift, 1))
    corr_ref[...] = correction
    length = loop_out.shape[2]
    away = lax.rem(N - blk * length, N)
    loop_out[0] = pltpu.roll(correction, away, 1)[:count, :length]

    for v in range(count):
        for a in range(FOLD):
            for b in range(FOLD):
                after = src[v, a // 2, b // 2]
                x = u2s[v, a // 2, b // 2]
                gain = (after[:R] - x[:R], after[R:] - narrow(x)[1])
                at = (v * FOLD + a) * FOLD + b
                k = (2 * count + 1) * 4 + at // R
                high = above[k, at % R : at % R + 1]
                low = below[k, at % R : at % R + 1]
                start[v, a, b, :R] = u1[v, a, b] + gain[0]
                start[v, a, b, R:] = jnp.where(sub < R // 2, high, low) + gain[1]
    lane = lanes_of(2 * R, J)
    ring = lanes_of(2 * R, N)
    last = jnp.logical_and(lane == J - 1, row == 0)
    first = jnp.logical_and(lane == 0, row == 1)
    for a in range(FOLD):
        match = cells[a, :, :1] == ring
        for v in range(count):
            fix = jnp.where(match, corr_ref[v : v + 1], 0.0)
            fix = jnp.sum(fix, axis=1, keepdims=True)
            start[v, a, FOLD - 1] = start[v, a, FOLD - 1] + jnp.where(last, fix, 0.0)
            start[v, a, 0] = start[v, a, 0] + jnp.where(first, fix, 0.0)
    src = start
    for k in range(SECTIONS1):
        dst = (buf_a, buf_b)[k % 2]
        rows = R if k == SECTIONS1 - 1 else 2 * R
        section(dst, src, start, source, sigma, 1.0, 1.0 / (SECTIONS1 - k), FOLD, rows)
        src = dst
    for v in range(count):
        for a in range(FOLD):
            for b in range(FOLD):
                stage[v, b, pl.ds(a, R, stride=FOLD), :] = src[v, a, b, :R]
        for c, x in enumerate(join_lanes([stage[v, b] for b in range(FOLD)])):
            solution_ref[0, v, :, c * J : (c + 1) * J] = x


def body(state, forcing, sigma, partner, loop_weight, offset):
    _, count, rows, cols = state.shape
    R, J = rows // FOLD, cols // FOLD
    N = loop_weight.shape[1]
    blocks = lax.axis_size("blk")
    length = N // blocks
    real = functools.partial(jax.ShapeDtypeStruct, dtype=jnp.float32)
    scratch = lambda *shape: pltpu.VMEM(shape, jnp.float32)
    deep = 2 * FOLD
    last = rows // deep - 1

    def ends(lead):
        zero = (0,) * len(lead)
        return [
            pl.BlockSpec(lead + (deep, cols), lambda i: zero + (0, 0)),
            pl.BlockSpec(lead + (deep, cols), lambda i: zero + (last, 0)),
        ]

    packed = real(((2 * count + 2) * FOLD, cols))
    whole = pl.BlockSpec(packed.shape, lambda i: (0, 0))
    head, tail = pl.pallas_call(
        pack_kernel,
        grid=(1,),
        in_specs=ends((1, count)) * 2 + ends((1,)) + [pl.BlockSpec((1, rows, 1), lambda i: (0, 0, 0))],
        out_specs=[whole, whole],
        out_shape=[packed, packed],
        name="pack",
    )(state, state, forcing, forcing, sigma, sigma, partner)
    up = [(i, (i + 1) % blocks) for i in range(blocks)]
    down = [((i + 1) % blocks, i) for i in range(blocks)]
    below = lax.ppermute(tail, "blk", up)
    above = lax.ppermute(head, "blk", down)

    st, fo, sg = pl.pallas_call(
        fold_kernel,
        in_specs=[vmem()] * 3,
        out_specs=[vmem()] * 3,
        out_shape=[
            real((count, FOLD, FOLD, R, J)),
            real((count, FOLD, FOLD, R, J)),
            real((FOLD, FOLD, R, J)),
        ],
        scratch_shapes=[scratch(2 * count + 1, FOLD, rows, J)],
        name="fold",
    )(state, forcing, sigma)

    tiles = (2 * count + 1) * 4
    message = real((tiles + count * FOLD * FOLD // R, R, J))
    fine = (count, FOLD, FOLD, 2 * R, J)
    u1, source, sigma_w, cells, head, tail, loop = pl.pallas_call(
        down_kernel,
        in_specs=[vmem()] * 6,
        out_specs=[vmem()] * 7,
        out_shape=[
            real((count, FOLD, FOLD, R, J)),
            real(fine),
            real((FOLD, FOLD, 2 * R, J)),
            jax.ShapeDtypeStruct((FOLD, 2 * R, J), jnp.int32),
            message,
            message,
            real((16, N)),
        ],
        scratch_shapes=[
            scratch(*fine),
            scratch(*fine),
            scratch(*fine),
            scratch(2 * count + 1, FOLD, 2 * FOLD, J),
            scratch(count, FOLD, FOLD, R, J),
            pltpu.VMEM((rows, J), jnp.int32),
        ],
        name="down",
    )(st, fo, sg, below, above, partner)

    below = lax.ppermute(tail, "blk", up)
    above = lax.ppermute(head, "blk", down)
    loop = loop + lax.ppermute(loop, "row", [(0, 1), (1, 0)])
    reach = 1
    while reach < blocks:
        loop = loop + lax.ppermute(loop, "blk", [(i, i ^ reach) for i in range(blocks)])
        reach *= 2

    mid = (count, 2, 2, 3 * R, J)
    low = (count, 1, 1, 3 * R, J)
    thin = (count, 2, 2, 2 * R, J)
    result, loop_out = pl.pallas_call(
        up_kernel,
        in_specs=[vmem()] * 9 + [pl.BlockSpec(memory_space=pltpu.SMEM)],
        out_specs=[vmem()] * 2,
        out_shape=[real(state.shape), real((1, count, length))],
        scratch_shapes=[
            scratch(*mid), scratch(*mid), scratch(*mid[1:]), scratch(*mid),
            scratch(*low), scratch(*low), scratch(*low[1:]), scratch(*low),
            scratch(*mid), scratch(*mid), scratch(*low), scratch(*low),
            scratch(*thin), scratch(*thin), scratch(*thin[1:]), scratch(*thin), scratch(*thin),
            scratch(*fine), scratch(*fine), scratch(*fine),
            scratch(8, N),
            scratch(count, FOLD, rows, J),
        ],
        name="up",
    )(head, below, above, u1, source, sigma_w, cells, loop, loop_weight, offset)
    return result, loop_out


def solution(mesh):
    placed = (
        P("row", None, "blk", None),
        P("row", None, "blk", None),
        P("row", "blk", None),
        P("row", "blk", None),
        P("row", None),
        P(),
    )
    return jax.shard_map(
        body,
        mesh=mesh,
        in_specs=placed,
        out_specs=(P("row", None, "blk", None), P("row", None, "blk")),
        check_vma=False,
    )
```

profile of v0, /device:TPU:0, one launch (start us, length us, event | category | flops | bytes accessed | tf_op | source)
XLA Modules:
  0.0 48.5 jit_solution(9017595117892105366)
XLA Ops:
  0.6 1.3 %copy.8.p_ref = s32[1,32,1]{2,1,0:T(8,128)} copy(s32[1,32,1]{1,2,0:T(1,128)} %param.9) | data formatting | bytes 256 | tf_op args[3]
  2.0 1.8 %pack.1 = (f32[48,512]{1,0:T(8,128)}, f32[48,512]{1,0:T(8,128)}) custom-call(f32[1,5,32,512]{3,2,1,0:T(8,128)} %s_tail.1, f32[1,5,32,512]{3,2,1,0:T(8,128)} %s_tail.1, f32[1,5,32,512]{3,2,1,0:T(8,128)} %f_tail.1, f32[1,5,32,512]{3,2,1,0:T(8,128)} %f_tail.1, f32[1,32,512]{2,1,0:T(8,128)} %g_tail.1, f32[1,32,512]{2,1,0:T(8,128)} %g_tail.1, s32[1,32,1]{2,1,0:T(8,128)} %copy.8.p_ref), custom_call_target="tpu_custom_call" | custom-call | tf_op jit(solution)/shard_map/pack/pallas_call | solution.py:399
  3.8 3.0 %collective-permute-start = (f32[48,512]{1,0:T(8,128)}, f32[48,512]{1,0:T(8,128)S(1)}, u32[]{:S(2)}, u32[]{:S(2)}) collective-permute-start(f32[48,512]{1,0:T(8,128)} %get-tuple-element.17), channel_id=1, source_target_pairs={{0,1},{1,2},{2,3},{3,4},{4,5},{5,6},{6,7},{7,8},{8,9},{9,10},{10,1... | collective-permute-start | bytes 294920 | tf_op jit(solution)/shard_map/ppermute | solution.py:409
  6.7 4.0 %collective-permute-start.1 = (f32[48,512]{1,0:T(8,128)}, f32[48,512]{1,0:T(8,128)S(1)}, u32[]{:S(2)}, u32[]{:S(2)}) collective-permute-start(f32[48,512]{1,0:T(8,128)} %get-tuple-element.18), channel_id=1, source_target_pairs={{1,0},{2,1},{3,2},{4,3},{5,4},{6,5},{7,6},{8,7},{9,8},{10,9},{11,1... | collective-permute-start | bytes 294920 | tf_op jit(solution)/shard_map/ppermute | solution.py:410
  10.7 2.8 %fold.1 = (f32[5,4,4,8,128]{4,3,2,1,0:T(8,128)}, f32[5,4,4,8,128]{4,3,2,1,0:T(8,128)}, f32[4,4,8,128]{3,2,1,0:T(8,128)}) custom-call(f32[1,5,32,512]{3,2,1,0:T(8,128)} %s_tail.1, f32[1,5,32,512]{3,2,1,0:T(8,128)} %f_tail.1, f32[1,32,512]{2,1,0:T(8,128)} %g_tail.1), custom_call_target="tpu_custom_call" | custom-call | tf_op jit(solution)/shard_map/fold/pallas_call | solution.py:412
  13.5 0.3 collective-permute-done.below
  13.8 0.0 copy-start.2
  13.8 0.0 collective-permute-done.1.above
  13.8 0.0 copy-start.3
  13.8 0.6 %copy-done.2 = f32[48,512]{1,0:T(8,128)} copy-done((f32[48,512]{1,0:T(8,128)}, f32[48,512]{1,0:T(8,128)S(1)}, u32[]{:S(2)}) %copy-start.2) | copy-done | bytes 98328
  14.4 0.1 copy-done.3
  14.5 3.3 %down.1 = (f32[5,4,4,8,128]{4,3,2,1,0:T(8,128)}, f32[5,4,4,16,128]{4,3,2,1,0:T(8,128)}, f32[4,4,16,128]{3,2,1,0:T(8,128)}, s32[4,16,128]{2,1,0:T(8,128)}, f32[54...) custom-call(f32[5,4,4,8,128]{4,3,2,1,0:T(8,128)} %get-tuple-element.14.st, ...), custom_call_target="tpu_custom_call" | custom-call | tf_op jit(solution)/shard_map/down/pallas_call | solution.py:428
  17.8 5.3 %collective-permute-start.3 = (f32[54,8,128]{2,1,0:T(8,128)}, f32[54,8,128]{2,1,0:T(8,128)S(1)}, u32[]{:S(2)}, u32[]{:S(2)}) collective-permute-start(f32[54,8,128]{2,1,0:T(8,128)} %get-tuple-element.19.own), channel_id=1, source_target_pairs={{1,0},{2,1},{3,2},{4,3},{5,4},{6,5},{7,6},{8,7},{9,8},{10,9},{11,1... | collective-permute-start | bytes 663560 | tf_op jit(solution)/shard_map/ppermute | solution.py:453
  23.0 0.0 collective-permute-start.2
  23.0 0.0 collective-permute-start.4
  23.0 1.4 %collective-permute-done.4 = f32[16,128]{1,0:T(8,128)S(1)} collective-permute-done((f32[16,128]{1,0:T(8,128)}, f32[16,128]{1,0:T(8,128)S(1)}, u32[]{:S(2)}, u32[]{:S(2)}) %collective-permute-start.4) | collective-permute-done | bytes 8224 | tf_op jit(solution)/shard_map/ppermute | solution.py:454
  24.4 0.7 %add.15 = f32[16,128]{1,0:T(8,128)S(1)} add(f32[16,128]{1,0:T(8,128)} %get-tuple-element.25, f32[16,128]{1,0:T(8,128)S(1)} %collective-permute-done.4) | non-fusion elementwise | flops 2048 | bytes 24576 | tf_op jit(solution)/shard_map/add | solution.py:454
  25.1 0.0 collective-permute-start.5
  25.1 4.3 %collective-permute-done.5 = f32[16,128]{1,0:T(8,128)S(1)} collective-permute-done((f32[16,128]{1,0:T(8,128)S(1)}, f32[16,128]{1,0:T(8,128)S(1)}, u32[]{:S(2)}, u32[]{:S(2)}) %collective-permute-start.5) | collective-permute-done | bytes 8224 | tf_op jit(solution)/shard_map/ppermute | solution.py:457
  29.4 0.0 collective-permute-start.6
  29.4 3.6 %collective-permute-done.6 = f32[16,128]{1,0:T(8,128)S(1)} collective-permute-done((f32[16,128]{1,0:T(8,128)S(1)}, f32[16,128]{1,0:T(8,128)S(1)}, u32[]{:S(2)}, u32[]{:S(2)}) %collective-permute-start.6) | collective-permute-done | bytes 8224 | tf_op jit(solution)/shard_map/ppermute | solution.py:457
  33.1 0.9 %collective-permute-start.7 = (f32[16,128]{1,0:T(8,128)S(1)}, f32[16,128]{1,0:T(8,128)S(1)}, u32[]{:S(2)}, u32[]{:S(2)}) collective-permute-start(f32[16,128]{1,0:T(8,128)S(1)} %add.17), channel_id=1, source_target_pairs={{0,4},{1,5},{2,6},{3,7},{4,0},{5,1},{6,2},{7,3},{8,12},{9,13},{10,... | collective-permute-start | bytes 24584 | tf_op jit(solution)/shard_map/ppermute | solution.py:457
  34.0 2.7 %collective-permute-done.7 = f32[16,128]{1,0:T(8,128)S(1)} collective-permute-done((f32[16,128]{1,0:T(8,128)S(1)}, f32[16,128]{1,0:T(8,128)S(1)}, u32[]{:S(2)}, u32[]{:S(2)}) %collective-permute-start.7) | collective-permute-done | bytes 8224 | tf_op jit(solution)/shard_map/ppermute | solution.py:457
  36.8 1.9 %collective-permute-start.8 = (f32[16,128]{1,0:T(8,128)S(1)}, f32[16,128]{1,0:T(8,128)S(1)}, u32[]{:S(2)}, u32[]{:S(2)}) collective-permute-start(f32[16,128]{1,0:T(8,128)S(1)} %add.18), channel_id=1, source_target_pairs={{0,8},{1,9},{2,10},{3,11},{4,12},{5,13},{6,14},{7,15},{8,0},{9,1},... | collective-permute-start | bytes 24584 | tf_op jit(solution)/shard_map/ppermute | solution.py:457
  39.3 2.0 %collective-permute-done.8 = f32[16,128]{1,0:T(8,128)S(1)} collective-permute-done((f32[16,128]{1,0:T(8,128)S(1)}, f32[16,128]{1,0:T(8,128)S(1)}, u32[]{:S(2)}, u32[]{:S(2)}) %collective-permute-start.8) | collective-permute-done | bytes 8224 | tf_op jit(solution)/shard_map/ppermute | solution.py:457
  41.3 0.6 %add.19.loop = f32[16,128]{1,0:T(8,128)} add(f32[16,128]{1,0:T(8,128)S(1)} %add.18, f32[16,128]{1,0:T(8,128)S(1)} %collective-permute-done.8) | non-fusion elementwise | flops 2048 | bytes 24576 | tf_op jit(solution)/shard_map/add | solution.py:457
  41.9 0.0 collective-permute-done.3.above
  41.9 0.0 copy-start
  41.9 0.0 collective-permute-done.2.below
  41.9 0.0 copy-start.1
  41.9 0.7 %copy-done = f32[54,8,128]{2,1,0:T(8,128)} copy-done((f32[54,8,128]{2,1,0:T(8,128)}, f32[54,8,128]{2,1,0:T(8,128)S(1)}, u32[]{:S(2)}) %copy-start) | copy-done | bytes 221208
  42.6 0.1 copy-done.1
  42.7 4.5 %up.1 = (f32[1,5,32,512]{3,2,1,0:T(8,128)}, f32[1,5,8]{2,1,0:T(8,128)}) custom-call(f32[54,8,128]{2,1,0:T(8,128)} %get-tuple-element.19.own, f32[54,8,128]{2,1,0:T(8,128)} %copy-done.1, f32[54,8,128]{2,1,0:T(8,128)} %copy-done, f32[5,4,4,8,128]{4,3,2,1,0:T(8,128)} %get-tuple-element.21.u1, f32[5,4,4,16,128]{4,3,2,1,0:T(8,128)} %get-tuple-element.22.source, ...), custom_call_target="tpu_custom_call" | custom-call | tf_op jit(solution)/shard_map/up/pallas_call | solution.py:463
  47.2 1.3 %copy.10 = f32[1,5,8]{2,0,1:T(1,128)} copy(f32[1,5,8]{2,1,0:T(8,128)} %get-tuple-element.27) | data formatting | bytes 320 | tf_op jit(solution)/shard_map/up/pallas_call | solution.py:463
  (3 shorter events, 0.0 us)
Async XLA Ops:
  3.8 10.1 %collective-permute-start = (f32[48,512]{1,0:T(8,128)}, f32[48,512]{1,0:T(8,128)S(1)}, u32[]{:S(2)}, u32[]{:S(2)}) collective-permute-start(f32[48,512]{1,0:T(8,128)} %get-tuple-element.17), channel_id=1, source_target_pairs={{0,1},{1,2},{2,3},{3,4},{4,5},{5,6},{6,7},{7,8},{8,9},{9,10},{10,1... | collective-permute-start | bytes 294920 | tf_op jit(solution)/shard_map/ppermute | solution.py:409
  6.7 7.1 %collective-permute-start.1 = (f32[48,512]{1,0:T(8,128)}, f32[48,512]{1,0:T(8,128)S(1)}, u32[]{:S(2)}, u32[]{:S(2)}) collective-permute-start(f32[48,512]{1,0:T(8,128)} %get-tuple-element.18), channel_id=1, source_target_pairs={{1,0},{2,1},{3,2},{4,3},{5,4},{6,5},{7,6},{8,7},{9,8},{10,9},{11,1... | collective-permute-start | bytes 294920 | tf_op jit(solution)/shard_map/ppermute | solution.py:410
  13.8 0.6 %copy-start.2 = (f32[48,512]{1,0:T(8,128)}, f32[48,512]{1,0:T(8,128)S(1)}, u32[]{:S(2)}) copy-start(f32[48,512]{1,0:T(8,128)S(1)} %collective-permute-done.below) | copy-start | bytes 294916
  13.8 0.7 %copy-start.3 = (f32[48,512]{1,0:T(8,128)}, f32[48,512]{1,0:T(8,128)S(1)}, u32[]{:S(2)}) copy-start(f32[48,512]{1,0:T(8,128)S(1)} %collective-permute-done.1.above) | copy-start | bytes 294916
  17.8 24.1 %collective-permute-start.3 = (f32[54,8,128]{2,1,0:T(8,128)}, f32[54,8,128]{2,1,0:T(8,128)S(1)}, u32[]{:S(2)}, u32[]{:S(2)}) collective-permute-start(f32[54,8,128]{2,1,0:T(8,128)} %get-tuple-element.19.own), channel_id=1, source_target_pairs={{1,0},{2,1},{3,2},{4,3},{5,4},{6,5},{7,6},{8,7},{9,8},{10,9},{11,1... | collective-permute-start | bytes 663560 | tf_op jit(solution)/shard_map/ppermute | solution.py:453
  23.0 18.9 %collective-permute-start.2 = (f32[54,8,128]{2,1,0:T(8,128)}, f32[54,8,128]{2,1,0:T(8,128)S(1)}, u32[]{:S(2)}, u32[]{:S(2)}) collective-permute-start(f32[54,8,128]{2,1,0:T(8,128)} %get-tuple-element.20), channel_id=1, source_target_pairs={{0,1},{1,2},{2,3},{3,4},{4,5},{5,6},{6,7},{7,8},{8,9},{9,10},{10,1... | collective-permute-start | bytes 663560 | tf_op jit(solution)/shard_map/ppermute | solution.py:452
  23.0 1.4 %collective-permute-start.4 = (f32[16,128]{1,0:T(8,128)}, f32[16,128]{1,0:T(8,128)S(1)}, u32[]{:S(2)}, u32[]{:S(2)}) collective-permute-start(f32[16,128]{1,0:T(8,128)} %get-tuple-element.25), channel_id=1, source_target_pairs={{0,16},{16,0},{1,17},{17,1},{2,18},{18,2},{3,19},{19,3},{4,20},{20... | collective-permute-start | bytes 24584 | tf_op jit(solution)/shard_map/ppermute | solution.py:454
  25.1 4.3 %collective-permute-start.5 = (f32[16,128]{1,0:T(8,128)S(1)}, f32[16,128]{1,0:T(8,128)S(1)}, u32[]{:S(2)}, u32[]{:S(2)}) collective-permute-start(f32[16,128]{1,0:T(8,128)S(1)} %add.15), channel_id=1, source_target_pairs={{0,1},{1,0},{2,3},{3,2},{4,5},{5,4},{6,7},{7,6},{8,9},{9,8},{10,11... | collective-permute-start | bytes 24584 | tf_op jit(solution)/shard_map/ppermute | solution.py:457
  29.4 3.7 %collective-permute-start.6 = (f32[16,128]{1,0:T(8,128)S(1)}, f32[16,128]{1,0:T(8,128)S(1)}, u32[]{:S(2)}, u32[]{:S(2)}) collective-permute-start(f32[16,128]{1,0:T(8,128)S(1)} %add.16), channel_id=1, source_target_pairs={{0,2},{1,3},{2,0},{3,1},{4,6},{5,7},{6,4},{7,5},{8,10},{9,11},{10,... | collective-permute-start | bytes 24584 | tf_op jit(solution)/shard_map/ppermute | solution.py:457
  33.1 3.7 %collective-permute-start.7 = (f32[16,128]{1,0:T(8,128)S(1)}, f32[16,128]{1,0:T(8,128)S(1)}, u32[]{:S(2)}, u32[]{:S(2)}) collective-permute-start(f32[16,128]{1,0:T(8,128)S(1)} %add.17), channel_id=1, source_target_pairs={{0,4},{1,5},{2,6},{3,7},{4,0},{5,1},{6,2},{7,3},{8,12},{9,13},{10,... | collective-permute-start | bytes 24584 | tf_op jit(solution)/shard_map/ppermute | solution.py:457
  36.8 4.5 %collective-permute-start.8 = (f32[16,128]{1,0:T(8,128)S(1)}, f32[16,128]{1,0:T(8,128)S(1)}, u32[]{:S(2)}, u32[]{:S(2)}) collective-permute-start(f32[16,128]{1,0:T(8,128)S(1)} %add.18), channel_id=1, source_target_pairs={{0,8},{1,9},{2,10},{3,11},{4,12},{5,13},{6,14},{7,15},{8,0},{9,1},... | collective-permute-start | bytes 24584 | tf_op jit(solution)/shard_map/ppermute | solution.py:457
  41.9 0.7 %copy-start = (f32[54,8,128]{2,1,0:T(8,128)}, f32[54,8,128]{2,1,0:T(8,128)S(1)}, u32[]{:S(2)}) copy-start(f32[54,8,128]{2,1,0:T(8,128)S(1)} %collective-permute-done.3.above) | copy-start | bytes 663556
  41.9 0.8 %copy-start.1 = (f32[54,8,128]{2,1,0:T(8,128)}, f32[54,8,128]{2,1,0:T(8,128)S(1)}, u32[]{:S(2)}) copy-start(f32[54,8,128]{2,1,0:T(8,128)S(1)} %collective-permute-done.2.below) | copy-start | bytes 663556
where the time goes:
time: 48.8 us; the launch traced here: 48.5 us
  starting transfers between devices  15.1 us (31%)
  waiting for transfers between devices  14.4 us (30%)
  Pallas kernels  12.3 us (25%)
  local copies, waits for them, and re-layouts  4.03 us (8%)
  between operations  1.31 us (3%)
  other arithmetic  1.3 us (3%)
    ppermute x4, waiting for transfers between devices, body(): lax.ppermute(loop, 'blk', [(i, i ^ reach) for i in range(blocks)])  12.7 us
    ppermute x2, starting transfers between devices, body(): above = lax.ppermute(head, 'blk', down)  9.27 us
    pallas_call x1, Pallas kernels, body(): pl.pallas_call(up_kernel, in_specs=[vmem()] * 9 + [pl.BlockSpec(memory_sp...  4.54 us
    pallas_call x1, Pallas kernels, body(): pl.pallas_call(down_kernel, in_specs=[vmem()] * 6, out_specs=[vmem()] * 7...  3.26 us
    ppermute x2, starting transfers between devices, body(): below = lax.ppermute(tail, 'blk', up)  2.97 us
    ppermute x4, starting transfers between devices, body(): lax.ppermute(loop, 'blk', [(i, i ^ reach) for i in range(blocks)])  2.87 us
    unnamed x9, local copies, waits for them, and re-layouts  2.77 us
    pallas_call x1, Pallas kernels, body(): pl.pallas_call(fold_kernel, in_specs=[vmem()] * 3, out_specs=[vmem()] * 3...  2.76 us
  transfers between devices with their start and end apart: 9, of which 6 were waited for; matrix products, arithmetic and copies ran while one was open for 3% of the time, Pallas kernels for 6%

commit v1 on v0

--- a/solution.py
+++ b/solution.py
@@ -7,12 +7,14 @@
 from jax.experimental.pallas import tpu as pltpu
 from jax.sharding import PartitionSpec as P
 
+
 SECTIONS1 = 3
 SECTIONS2 = 3
 SECTIONS3 = 4
 COEFF = 0.8
 
 FOLD = 4
+LIMIT = 24 * 1024 * 1024
 
 
 def vmem():
@@ -118,50 +120,75 @@
     return x & (size - 1) if size & (size - 1) == 0 else lax.rem(x, size)
 
 
-def pack_kernel(s_head, s_tail, f_head, f_tail, g_head, g_tail, p_ref, head, tail):
-    count = s_head.shape[1]
-    rows = p_ref.shape[1]
-    cols = head.shape[1]
+def fetch(pairs, sems):
+    copies = [pltpu.make_async_copy(x, y, sems.at[k]) for k, (x, y) in enumerate(pairs)]
+    for copy in copies:
+        copy.start()
+    for copy in copies:
+        copy.wait()
+
+
+def pack_kernel(s_ref, f_ref, g_ref, p_ref, head, tail, s_end, f_end, g_end, slots, sems):
+    count, rows = s_ref.shape[1:3]
     edge = FOLD
-    deep = s_tail.shape[2]
-    for v in range(count):
-        for k, (top, bottom) in enumerate(((s_head, s_tail), (f_head, f_tail))):
-            at = (k * count + v) * edge
-            head[at : at + edge] = top[0, v, :edge]
-            tail[at : at + edge] = bottom[0, v, deep - edge :]
-    at = 2 * count * edge
-    head[at : at + edge] = g_head[0, :edge]
-    tail[at : at + edge] = g_tail[0, deep - edge :]
-    at += edge
-    head[at : at + edge] = jnp.broadcast_to(p_ref[0, :edge].astype(jnp.float32), (edge, cols))
-    tail[at : at + edge] = jnp.broadcast_to(p_ref[0, rows - edge :].astype(jnp.float32), (edge, cols))
-
-
-def fold_kernel(s_ref, f_ref, g_ref, st, fo, sg, stage):
-    rows = st.shape[-2]
+    deep = 2 * edge
+    parts = (slice(0, deep), slice(rows - deep, rows))
+    pairs = [(p_ref, slots)]
+    for k, part in enumerate(parts):
+        pairs += [
+            (s_ref.at[0, :, part], s_end.at[k]),
+            (f_ref.at[0, :, part], f_end.at[k]),
+            (g_ref.at[0, part], g_end.at[k]),
+        ]
+    fetch(pairs, sems)
+    for k, message in enumerate((head, tail)):
+        keep = slice(0, edge) if k == 0 else slice(deep - edge, deep)
+        for v in range(count):
+            message[v * edge : (v + 1) * edge] = s_end[k, v, keep]
+            message[(count + v) * edge : (count + v + 1) * edge] = f_end[k, v, keep]
+        at = 2 * count * edge
+        message[at : at + edge] = g_end[k, keep]
+        at += edge
+        message[at : at + edge] = jnp.zeros((edge, message.shape[1]), jnp.float32)
+        message[at : at + 1, :rows] = slots[...].astype(jnp.float32)
+
+
+def fold_kernel(
+    s_hbm, f_hbm, g_hbm, p_hbm, st, fo, sg, own_slot,
+    s_ref, f_ref, g_ref, p_ref, stage, slots, sems,
+):
     count = st.shape[0]
+    R, _ = st.shape[-2:]
+    rows = s_hbm.shape[2]
+    fetch(((s_hbm.at[0], s_ref), (f_hbm.at[0], f_ref), (g_hbm.at[0], g_ref), (p_hbm, p_ref)), sems)
     for ch in range(2 * count + 1):
         kind, v = divmod(ch, count)
-        x = g_ref[0] if kind == 2 else (s_ref, f_ref)[kind][0, v]
+        x = g_ref[...] if kind == 2 else (s_ref, f_ref)[kind][v]
         for b, part in enumerate(split_lanes(x)):
             stage[ch, b] = part
         for a in range(FOLD):
             for b in range(FOLD):
-                part = stage[ch, b, pl.ds(a, rows, stride=FOLD), :]
+                part = stage[ch, b, pl.ds(a, R, stride=FOLD), :]
                 if kind == 2:
                     sg[a, b] = part
                 else:
                     (st, fo)[kind][v, a, b] = part
+    diagonal = lanes_of(rows, rows) == rows_of(rows, rows)
+    column = jnp.where(diagonal, p_ref[...].astype(jnp.float32), 0.0)
+    column = jnp.sum(column, axis=1, keepdims=True).astype(jnp.int32)
+    slots[...] = jnp.broadcast_to(column, slots.shape)
+    for a in range(FOLD):
+        own_slot[a] = slots[pl.ds(a, R, stride=FOLD), :]
 
 
 def down_kernel(
-    st, fo, sg, below, above, p_ref,
+    st, fo, sg, own_slot, below, above,
     u1, source, sigma, cells, head, tail, loop,
-    start, buf_a, buf_b, edge_buf, resid, own_slot,
+    start, buf_a, buf_b, edge_buf, resid, own_loop,
 ):
     count = st.shape[0]
     R, J = st.shape[-2:]
-    N = loop.shape[1]
+    N = loop.shape[2]
     edge = FOLD
     row = lax.axis_index("row")
     blk = lax.axis_index("blk")
@@ -179,7 +206,14 @@
         high = edge_buf[ch, b, edge + a : edge + a + 1]
         return jnp.where(sub == 0, high, jnp.where(sub == R - 1, low, 0.0))
 
-    own_slot[...] = jnp.broadcast_to(p_ref[0], own_slot.shape)
+    rows = R * FOLD
+    at = (2 * count + 1) * edge
+    place = lanes_of(1, rows)
+
+    def slot_of(message, i):
+        x = jnp.where(place == i, message[at : at + 1, :rows], 0.0)
+        return jnp.sum(x, axis=1, keepdims=True).astype(jnp.int32)
+
     for a in range(FOLD):
         for b in range(FOLD):
             for v in range(count):
@@ -189,10 +223,9 @@
                 source[v, a, b, R:] = halo(count + v, a, b)
             sigma[a, b, :R] = sg[a, b]
             sigma[a, b, R:] = halo(2 * count, a, b)
-        at = (2 * count + 1) * edge + a
-        own = own_slot[pl.ds(a, R, stride=FOLD), :]
-        low = below[at : at + 1, :J].astype(jnp.int32)
-        high = above[at : at + 1, :J].astype(jnp.int32)
+        own = own_slot[a]
+        low = jnp.broadcast_to(slot_of(below, rows - edge + a), (R, J))
+        high = jnp.broadcast_to(slot_of(above, a), (R, J))
         cells[a, :R] = wrap(own * blocks + blk, N)
         cells[a, R:] = jnp.where(
             sub < R // 2,
@@ -243,27 +276,26 @@
             face = jnp.where(row == 0, resid[v, a, FOLD - 1], resid[v, a, 0])
             face = jnp.sum(jnp.where(lane == column, face, 0.0), axis=1, keepdims=True)
             sums[v] = sums[v] + jnp.where(match, face, 0.0)
-    loop[...] = jnp.zeros_like(loop)
-    half = loop.shape[0] // 2
-    for v in range(count):
-        total = jnp.sum(sums[v], axis=0, keepdims=True)
-        for r in range(2):
-            at = r * half + v
-            loop[at : at + 1] = jnp.where(row == r, total, 0.0)
+    own_loop[...] = jnp.zeros_like(own_loop)
+    for v in range(count):
+        own_loop[v : v + 1] = jnp.sum(sums[v], axis=0, keepdims=True)
+    loop[...] = jnp.broadcast_to(own_loop[...][None], loop.shape)
 
 
 def up_kernel(
-    own, below, above, u1, source, sigma, cells, loop, weight_ref, offset_ref,
+    own, below, above, u1, source, sigma, cells, loop, weight_hbm, offset_ref,
     solution_ref, loop_out,
     u2s, r2s, s2, f2, u3s, r3s, s3, f3, buf2a, buf2b, buf3a, buf3b,
-    n2, nf2, ns2, nu2s, nb2, start, buf_a, buf_b, corr_ref, stage,
+    n2, nf2, ns2, nu2s, nb2, start, buf_a, buf_b, corr_ref, stage, weight_ref, sem,
 ):
     count = u1.shape[0]
     R, J = u1.shape[-2:]
-    N = loop.shape[1]
+    N = loop.shape[2]
     row = lax.axis_index("row")
     blk = lax.axis_index("blk")
     sub = rows_of(R, J)
+    weights = pltpu.make_async_copy(weight_hbm, weight_ref, sem)
+    weights.start()
 
     for at in range(8 * count + 4):
         if at < 8 * count:
@@ -321,7 +353,7 @@
                     nf2[v, a, b, at] = narrow(f2[v, a, b])[part]
                     if v == 0:
                         ns2[a, b, at] = narrow(s2[a, b])[part]
-    src, other = n2, nb2
+    src = n2
     spare = nu2s
     for k in range(SECTIONS2):
         dst = (nb2, spare)[k % 2]
@@ -329,15 +361,20 @@
         src = dst
 
     half = loop.shape[0] // 2
-    mine = jnp.where(row == 0, loop[:half], loop[half:])
-    others = jnp.where(row == 0, loop[half:], loop[:half])
+    rotor = jnp.sum(loop[:half], axis=0)
+    stator = jnp.sum(loop[half:], axis=0)
+    mine = jnp.where(row == 0, rotor, stator)
+    others = jnp.where(row == 0, stator, rotor)
     offset = offset_ref[0]
+    weights.wait()
     shift = lax.rem(jnp.where(row == 0, N - offset, offset), N)
     correction = weight_ref[...] * (mine + pltpu.roll(others, shift, 1))
     corr_ref[...] = correction
     length = loop_out.shape[2]
     away = lax.rem(N - blk * length, N)
-    loop_out[0] = pltpu.roll(correction, away, 1)[:count, :length]
+    shown = pltpu.roll(correction, away, 1)
+    for v in range(count):
+        loop_out[v] = shown[v : v + 1, :length]
 
     for v in range(count):
         for a in range(FOLD):
@@ -383,60 +420,73 @@
     blocks = lax.axis_size("blk")
     length = N // blocks
     real = functools.partial(jax.ShapeDtypeStruct, dtype=jnp.float32)
+    near = lambda shape, dtype=jnp.float32: pltpu.VMEM(shape, dtype)
+    away = lambda x: pltpu.with_memory_space_constraint(x, pltpu.HBM)
+    held = lambda x: pltpu.with_memory_space_constraint(x, pltpu.VMEM)
     scratch = lambda *shape: pltpu.VMEM(shape, jnp.float32)
+    far = pl.BlockSpec(memory_space=pltpu.HBM)
     deep = 2 * FOLD
-    last = rows // deep - 1
-
-    def ends(lead):
-        zero = (0,) * len(lead)
-        return [
-            pl.BlockSpec(lead + (deep, cols), lambda i: zero + (0, 0)),
-            pl.BlockSpec(lead + (deep, cols), lambda i: zero + (last, 0)),
-        ]
-
-    packed = real(((2 * count + 2) * FOLD, cols))
-    whole = pl.BlockSpec(packed.shape, lambda i: (0, 0))
+    slots = partner[:, :, 0]
+    packed = near(((2 * count + 2) * FOLD, cols))
+    limit = pltpu.CompilerParams(vmem_limit_bytes=LIMIT)
     head, tail = pl.pallas_call(
         pack_kernel,
-        grid=(1,),
-        in_specs=ends((1, count)) * 2 + ends((1,)) + [pl.BlockSpec((1, rows, 1), lambda i: (0, 0, 0))],
-        out_specs=[whole, whole],
+        in_specs=[far] * 4,
+        out_specs=[vmem()] * 2,
         out_shape=[packed, packed],
+        scratch_shapes=[
+            scratch(2, count, deep, cols),
+            scratch(2, count, deep, cols),
+            scratch(2, deep, cols),
+            pltpu.VMEM((1, rows), jnp.int32),
+            pltpu.SemaphoreType.DMA((7,)),
+        ],
+        compiler_params=limit,
         name="pack",
-    )(state, state, forcing, forcing, sigma, sigma, partner)
+    )(away(state), away(forcing), away(sigma), away(slots))
     up = [(i, (i + 1) % blocks) for i in range(blocks)]
     down = [((i + 1) % blocks, i) for i in range(blocks)]
     below = lax.ppermute(tail, "blk", up)
     above = lax.ppermute(head, "blk", down)
 
-    st, fo, sg = pl.pallas_call(
+    st, fo, sg, own_slot = pl.pallas_call(
         fold_kernel,
-        in_specs=[vmem()] * 3,
-        out_specs=[vmem()] * 3,
+        in_specs=[far] * 4,
+        out_specs=[vmem()] * 4,
         out_shape=[
-            real((count, FOLD, FOLD, R, J)),
-            real((count, FOLD, FOLD, R, J)),
-            real((FOLD, FOLD, R, J)),
+            near((count, FOLD, FOLD, R, J)),
+            near((count, FOLD, FOLD, R, J)),
+            near((FOLD, FOLD, R, J)),
+            near((FOLD, R, J), jnp.int32),
         ],
-        scratch_shapes=[scratch(2 * count + 1, FOLD, rows, J)],
+        scratch_shapes=[
+            scratch(count, rows, cols),
+            scratch(count, rows, cols),
+            scratch(rows, cols),
+            pltpu.VMEM((1, rows), jnp.int32),
+            scratch(2 * count + 1, FOLD, rows, J),
+            pltpu.VMEM((rows, J), jnp.int32),
+            pltpu.SemaphoreType.DMA((4,)),
+        ],
+        compiler_params=limit,
         name="fold",
-    )(state, forcing, sigma)
+    )(away(state), away(forcing), away(sigma), away(slots))
 
     tiles = (2 * count + 1) * 4
-    message = real((tiles + count * FOLD * FOLD // R, R, J))
+    message = near((tiles + count * FOLD * FOLD // R, R, J))
     fine = (count, FOLD, FOLD, 2 * R, J)
     u1, source, sigma_w, cells, head, tail, loop = pl.pallas_call(
         down_kernel,
         in_specs=[vmem()] * 6,
         out_specs=[vmem()] * 7,
         out_shape=[
-            real((count, FOLD, FOLD, R, J)),
-            real(fine),
-            real((FOLD, FOLD, 2 * R, J)),
-            jax.ShapeDtypeStruct((FOLD, 2 * R, J), jnp.int32),
+            near((count, FOLD, FOLD, R, J)),
+            near(fine),
+            near((FOLD, FOLD, 2 * R, J)),
+            near((FOLD, 2 * R, J), jnp.int32),
             message,
             message,
-            real((16, N)),
+            near((2 * blocks, 8, N)),
         ],
         scratch_shapes=[
             scratch(*fine),
@@ -444,27 +494,24 @@
             scratch(*fine),
             scratch(2 * count + 1, FOLD, 2 * FOLD, J),
             scratch(count, FOLD, FOLD, R, J),
-            pltpu.VMEM((rows, J), jnp.int32),
+            scratch(8, N),
         ],
+        compiler_params=limit,
         name="down",
-    )(st, fo, sg, below, above, partner)
+    )(held(st), held(fo), held(sg), held(own_slot), held(below), held(above))
 
     below = lax.ppermute(tail, "blk", up)
     above = lax.ppermute(head, "blk", down)
-    loop = loop + lax.ppermute(loop, "row", [(0, 1), (1, 0)])
-    reach = 1
-    while reach < blocks:
-        loop = loop + lax.ppermute(loop, "blk", [(i, i ^ reach) for i in range(blocks)])
-        reach *= 2
+    loop = lax.all_to_all(loop, ("row", "blk"), 0, 0, tiled=True)
 
     mid = (count, 2, 2, 3 * R, J)
     low = (count, 1, 1, 3 * R, J)
     thin = (count, 2, 2, 2 * R, J)
     result, loop_out = pl.pallas_call(
         up_kernel,
-        in_specs=[vmem()] * 9 + [pl.BlockSpec(memory_space=pltpu.SMEM)],
+        in_specs=[vmem()] * 8 + [far, pl.BlockSpec(memory_space=pltpu.SMEM)],
         out_specs=[vmem()] * 2,
-        out_shape=[real(state.shape), real((1, count, length))],
+        out_shape=[real(state.shape), real((count, 1, length))],
         scratch_shapes=[
             scratch(*mid), scratch(*mid), scratch(*mid[1:]), scratch(*mid),
             scratch(*low), scratch(*low), scratch(*low[1:]), scratch(*low),
@@ -473,10 +520,16 @@
             scratch(*fine), scratch(*fine), scratch(*fine),
             scratch(8, N),
             scratch(count, FOLD, rows, J),
+            scratch(1, N),
+            pltpu.SemaphoreType.DMA(()),
         ],
+        compiler_params=limit,
         name="up",
-    )(head, below, above, u1, source, sigma_w, cells, loop, loop_weight, offset)
-    return result, loop_out
+    )(
+        held(head), held(below), held(above), held(u1), held(source), held(sigma_w), held(cells),
+        held(loop), away(loop_weight), offset,
+    )
+    return result, jnp.transpose(loop_out, (1, 0, 2))
 
 
 def solution(mesh):
@@ -488,6 +541,7 @@
         P("row", None),
         P(),
     )
+
     return jax.shard_map(
         body,
         mesh=mesh,

time: 48.8 us -> 39.4 us (0.81)
  local copies, waits for them, and re-layouts: 4.03 us -> 0 us
  Pallas kernels: 12.3 us -> 8.66 us
  waiting for transfers between devices: 14.4 us -> 10.8 us
  starting transfers between devices: 15.1 us -> 18.3 us
  other arithmetic: 1.3 us -> 0 us
    ppermute x5 -> x0, waiting for transfers between devices: 14 us -> none  [the longest x4 12.7 us: body(): lax.ppermute(loop, 'blk', [(i, i ^ reach) for i in range(blocks)])]
    ppermute x2, waiting for transfers between devices: 0.34 us -> 6.48 us  [body(): below = lax.ppermute(tail, 'blk', up)]
    all_to_all x0 -> x1, starting transfers between devices: none -> 5.74 us  [body(): loop = lax.all_to_all(loop, ('row', 'blk'), 0, 0, tiled=True)]
    ppermute x2, waiting for transfers between devices: 0.01 us -> 4.32 us  [body(): above = lax.ppermute(head, 'blk', down)]
    ppermute x5 -> x0, starting transfers between devices: 2.87 us -> none  [the longest x4 2.87 us: body(): lax.ppermute(loop, 'blk', [(i, i ^ reach) for i in range(blocks)])]
    unnamed x9 -> x0, local copies, waits for them, and re-layouts: 2.77 us -> none
    pallas_call x3, Pallas kernels: 9.08 us -> 6.53 us  [the longest x1 3.25 us: body(): pl.pallas_call(up_kernel, in_specs=[vmem()] * 8 + [far, pl.BlockSpec(memo...]
    add x5 -> x0, other arithmetic: 1.3 us -> none  [the longest x1 0.7 us: body(): loop = loop + lax.ppermute(loop, 'row', [(0, 1), (1, 0)])]
  transfers between devices with their start and end apart: 9 -> 5, of which waited for: 6 -> 3; matrix products, arithmetic and copies ran while one was open for 3% -> 0% of each run, Pallas kernels for 6% -> 5%
where the time goes in v1:
time: 39.4 us; the launch traced here: 39.1 us
  starting transfers between devices  18.3 us (46%)
  waiting for transfers between devices  10.8 us (27%)
  Pallas kernels  8.66 us (22%)
  between operations  1.31 us (3%)
    ppermute x2, starting transfers between devices, body(): above = lax.ppermute(head, 'blk', down)  9.58 us
    ppermute x2, waiting for transfers between devices, body(): below = lax.ppermute(tail, 'blk', up)  6.48 us
    all_to_all x1, starting transfers between devices, body(): loop = lax.all_to_all(loop, ('row', 'blk'), 0, 0, tiled=True)  5.74 us
    ppermute x2, waiting for transfers between devices, body(): above = lax.ppermute(head, 'blk', down)  4.32 us
    pallas_call x1, Pallas kernels, body(): pl.pallas_call(up_kernel, in_specs=[vmem()] * 8 + [far, pl.BlockSpec(memo...  3.25 us
    ppermute x2, starting transfers between devices, body(): below = lax.ppermute(tail, 'blk', up)  3.02 us
    pallas_call x1, Pallas kernels, body(): pl.pallas_call(fold_kernel, in_specs=[far] * 4, out_specs=[vmem()] * 4, o...  2.14 us
    pallas_call x1, Pallas kernels, body(): pl.pallas_call(down_kernel, in_specs=[vmem()] * 6, out_specs=[vmem()] * 7...  2.14 us
  transfers between devices with their start and end apart: 5, of which 3 were waited for; matrix products, arithmetic and copies ran while one was open for 0% of the time, Pallas kernels for 5%

profile of v1, /device:TPU:0, one launch (start us, length us, event | category | flops | bytes accessed | tf_op | source)
XLA Modules:
  0.0 39.1 jit_solution(5709376049582843987)
XLA Ops:
  0.6 1.1 %pack.1 = (f32[48,512]{1,0:T(8,128)S(1)}, f32[48,512]{1,0:T(8,128)S(1)}) custom-call(f32[1,5,32,512]{3,2,1,0:T(8,128)} %s_ref.1, f32[1,5,32,512]{3,2,1,0:T(8,128)} %f_ref.1, f32[1,32,512]{2,1,0:T(8,128)} %g_ref.1, s32[1,32]{1,0:T(1,128)} %bitcast.2), custom_call_target="tpu_custom_call" | custom-call | tf_op jit(solution)/shard_map/pack/pallas_call | solution.py:432
  1.8 3.0 %collective-permute-start = (f32[48,512]{1,0:T(8,128)S(1)}, f32[48,512]{1,0:T(8,128)S(1)}, u32[]{:S(2)}, u32[]{:S(2)}) collective-permute-start(f32[48,512]{1,0:T(8,128)S(1)} %get-tuple-element.21), channel_id=1, source_target_pairs={{0,1},{1,2},{2,3},{3,4},{4,5},{5,6},{6,7},{7,8},{8,9},{9,10},{10,1... | collective-permute-start | bytes 294920 | tf_op jit(solution)/shard_map/ppermute | solution.py:449
  4.8 4.1 %collective-permute-start.1 = (f32[48,512]{1,0:T(8,128)S(1)}, f32[48,512]{1,0:T(8,128)S(1)}, u32[]{:S(2)}, u32[]{:S(2)}) collective-permute-start(f32[48,512]{1,0:T(8,128)S(1)} %get-tuple-element.22), channel_id=1, source_target_pairs={{1,0},{2,1},{3,2},{4,3},{5,4},{6,5},{7,6},{8,7},{9,8},{10,9},{11,1... | collective-permute-start | bytes 294920 | tf_op jit(solution)/shard_map/ppermute | solution.py:450
  8.9 2.1 %fold.1 = (f32[5,4,4,8,128]{4,3,2,1,0:T(8,128)S(1)}, f32[5,4,4,8,128]{4,3,2,1,0:T(8,128)S(1)}, f32[4,4,8,128]{3,2,1,0:T(8,128)S(1)}, s32[4,8,128]{2,1,0:T(8,128)S(1)}) custom-call(f32[1,5,32,512]{3,2,1,0:T(8,128)} %s_ref.1, f32[1,5,32,512]{3,2,1,0:T(8,128)} %f_ref.1, f32[1,32,512]{2,1,0:T(8,128)} %g_ref.1, s32[1,32]{1,0:T(1,128)} %bitcast.3), custom_call_target="tpu_custom_call" | custom-call | tf_op jit(solution)/shard_map/fold/pallas_call | solution.py:452
  11.0 0.7 %collective-permute-done.below = f32[48,512]{1,0:T(8,128)S(1)} collective-permute-done((f32[48,512]{1,0:T(8,128)S(1)}, f32[48,512]{1,0:T(8,128)S(1)}, u32[]{:S(2)}, u32[]{:S(2)}) %collective-permute-start) | collective-permute-done | bytes 98336 | tf_op jit(solution)/shard_map/ppermute | solution.py:449
  11.7 0.0 collective-permute-done.1.above
  11.7 2.1 %down.1 = (f32[5,4,4,8,128]{4,3,2,1,0:T(8,128)S(1)}, f32[5,4,4,16,128]{4,3,2,1,0:T(8,128)S(1)}, f32[4,4,16,128]{3,2,1,0:T(8,128)S(1)}, s32[4,16,128]{2,1,0:T(8,1...) custom-call(f32[5,4,4,8,128]{4,3,2,1,0:T(8,128)S(1)} %get-tuple-element.17.st, ...), custom_call_target="tpu_custom_call" | custom-call | tf_op jit(solution)/shard_map/down/pallas_call | solution.py:478
  13.8 5.7 %all-to-all-start = ((f32[32,8,128]{2,1,0:T(8,128)}), f32[32,8,128]{2,1,0:T(8,128)S(1)}, u32[]{:S(2)}, u32[]{:S(2)}) async-start(f32[32,8,128]{2,1,0:T(8,128)} %get-tuple-element.29), calls=%async_computation | async-start | bytes 262144 | tf_op jit(solution)/shard_map/all_to_all | solution.py:505
  19.6 5.5 %collective-permute-start.3 = (f32[54,8,128]{2,1,0:T(8,128)S(1)}, f32[54,8,128]{2,1,0:T(8,128)S(1)}, u32[]{:S(2)}, u32[]{:S(2)}) collective-permute-start(f32[54,8,128]{2,1,0:T(8,128)S(1)} %get-tuple-element.23.own), channel_id=1, source_target_pairs={{1,0},{2,1},{3,2},{4,3},{5,4},{6,5},{7,6},{8,7},{9,8},{10,9},{11,1... | collective-permute-start | bytes 663560 | tf_op jit(solution)/shard_map/ppermute | solution.py:504
  25.1 0.0 collective-permute-start.2
  25.8 4.3 %collective-permute-done.3.above = f32[54,8,128]{2,1,0:T(8,128)S(1)} collective-permute-done((f32[54,8,128]{2,1,0:T(8,128)S(1)}, f32[54,8,128]{2,1,0:T(8,128)S(1)}, u32[]{:S(2)}, u32[]{:S(2)}) %collective-permute-start.3) | collective-permute-done | bytes 221216 | tf_op jit(solution)/shard_map/ppermute | solution.py:504
  30.1 5.8 %collective-permute-done.2.below = f32[54,8,128]{2,1,0:T(8,128)S(1)} collective-permute-done((f32[54,8,128]{2,1,0:T(8,128)S(1)}, f32[54,8,128]{2,1,0:T(8,128)S(1)}, u32[]{:S(2)}, u32[]{:S(2)}) %collective-permute-start.2) | collective-permute-done | bytes 221216 | tf_op jit(solution)/shard_map/ppermute | solution.py:503
  35.9 0.0 all-to-all-done.loop
  35.9 3.2 %up.1 = (f32[1,5,32,512]{3,2,1,0:T(8,128)}, f32[5,1,8]{2,1,0:T(1,128)}) custom-call(f32[54,8,128]{2,1,0:T(8,128)S(1)} %get-tuple-element.23.own, f32[54,8,128]{2,1,0:T(8,128)S(1)} %collective-permute-done.2.below, f32[54,8,128]{2,1,0:T(8,128)S(1)} %collective-permute-done.3.above, f32[5,4,4,8,128]{4,3,2,1,0:T(8,128)S(1)} %get-tuple-element.25.u1, ...), custom_call_target="tpu_custom_call" | custom-call | tf_op jit(solution)/shard_map/up/pallas_call | solution.py:510
Async XLA Ops:
  1.8 9.9 %collective-permute-start = (f32[48,512]{1,0:T(8,128)S(1)}, f32[48,512]{1,0:T(8,128)S(1)}, u32[]{:S(2)}, u32[]{:S(2)}) collective-permute-start(f32[48,512]{1,0:T(8,128)S(1)} %get-tuple-element.21), channel_id=1, source_target_pairs={{0,1},{1,2},{2,3},{3,4},{4,5},{5,6},{6,7},{7,8},{8,9},{9,10},{10,1... | collective-permute-start | bytes 294920 | tf_op jit(solution)/shard_map/ppermute | solution.py:449
  4.8 6.9 %collective-permute-start.1 = (f32[48,512]{1,0:T(8,128)S(1)}, f32[48,512]{1,0:T(8,128)S(1)}, u32[]{:S(2)}, u32[]{:S(2)}) collective-permute-start(f32[48,512]{1,0:T(8,128)S(1)} %get-tuple-element.22), channel_id=1, source_target_pairs={{1,0},{2,1},{3,2},{4,3},{5,4},{6,5},{7,6},{8,7},{9,8},{10,9},{11,1... | collective-permute-start | bytes 294920 | tf_op jit(solution)/shard_map/ppermute | solution.py:450
  13.8 22.0 %all-to-all-start = ((f32[32,8,128]{2,1,0:T(8,128)}), f32[32,8,128]{2,1,0:T(8,128)S(1)}, u32[]{:S(2)}, u32[]{:S(2)}) async-start(f32[32,8,128]{2,1,0:T(8,128)} %get-tuple-element.29), calls=%async_computation | async-start | bytes 262144 | tf_op jit(solution)/shard_map/all_to_all | solution.py:505
  19.6 10.5 %collective-permute-start.3 = (f32[54,8,128]{2,1,0:T(8,128)S(1)}, f32[54,8,128]{2,1,0:T(8,128)S(1)}, u32[]{:S(2)}, u32[]{:S(2)}) collective-permute-start(f32[54,8,128]{2,1,0:T(8,128)S(1)} %get-tuple-element.23.own), channel_id=1, source_target_pairs={{1,0},{2,1},{3,2},{4,3},{5,4},{6,5},{7,6},{8,7},{9,8},{10,9},{11,1... | collective-permute-start | bytes 663560 | tf_op jit(solution)/shard_map/ppermute | solution.py:504
  25.1 10.8 %collective-permute-start.2 = (f32[54,8,128]{2,1,0:T(8,128)S(1)}, f32[54,8,128]{2,1,0:T(8,128)S(1)}, u32[]{:S(2)}, u32[]{:S(2)}) collective-permute-start(f32[54,8,128]{2,1,0:T(8,128)S(1)} %get-tuple-element.24), channel_id=1, source_target_pairs={{0,1},{1,2},{2,3},{3,4},{4,5},{5,6},{6,7},{7,8},{8,9},{9,10},{10,1... | collective-permute-start | bytes 663560 | tf_op jit(solution)/shard_map/ppermute | solution.py:503

commit v2 on v1

--- a/solution.py
+++ b/solution.py
@@ -128,39 +128,33 @@
         copy.wait()
 
 
-def pack_kernel(s_ref, f_ref, g_ref, p_ref, head, tail, s_end, f_end, g_end, slots, sems):
-    count, rows = s_ref.shape[1:3]
-    edge = FOLD
-    deep = 2 * edge
-    parts = (slice(0, deep), slice(rows - deep, rows))
-    pairs = [(p_ref, slots)]
-    for k, part in enumerate(parts):
-        pairs += [
-            (s_ref.at[0, :, part], s_end.at[k]),
-            (f_ref.at[0, :, part], f_end.at[k]),
-            (g_ref.at[0, part], g_end.at[k]),
-        ]
-    fetch(pairs, sems)
-    for k, message in enumerate((head, tail)):
-        keep = slice(0, edge) if k == 0 else slice(deep - edge, deep)
-        for v in range(count):
-            message[v * edge : (v + 1) * edge] = s_end[k, v, keep]
-            message[(count + v) * edge : (count + v + 1) * edge] = f_end[k, v, keep]
-        at = 2 * count * edge
-        message[at : at + edge] = g_end[k, keep]
-        at += edge
-        message[at : at + edge] = jnp.zeros((edge, message.shape[1]), jnp.float32)
-        message[at : at + 1, :rows] = slots[...].astype(jnp.float32)
-
-
-def fold_kernel(
-    s_hbm, f_hbm, g_hbm, p_hbm, st, fo, sg, own_slot,
-    s_ref, f_ref, g_ref, p_ref, stage, slots, sems,
-):
+def edge_rows(count):
+    out = []
+    at = 0
+    for kind, width in ((0, SECTIONS1 + 1), (1, SECTIONS1), (2, SECTIONS1)):
+        for v in range(1 if kind == 2 else count):
+            out.append((kind, v, at, width))
+            at += width
+    return out, at
+
+
+def pack_kernel(s_hbm, f_hbm, g_hbm, p_hbm, head, tail, s_ref, f_ref, g_ref, p_ref, sems):
+    count, rows = s_ref.shape[:2]
+    fetch(((p_hbm, p_ref), (s_hbm.at[0], s_ref), (f_hbm.at[0], f_ref), (g_hbm.at[0], g_ref)), sems)
+    places, end = edge_rows(count)
+    for kind, v, at, width in places:
+        x = g_ref if kind == 2 else (s_ref, f_ref)[kind].at[v]
+        head[at : at + width] = x[:width]
+        tail[at : at + width] = x[rows - width :]
+    for message in (head, tail):
+        message[end:] = jnp.zeros((message.shape[0] - end, message.shape[1]), jnp.float32)
+        message[end : end + 1, :rows] = p_ref[...].astype(jnp.float32)
+
+
+def fold_kernel(s_ref, f_ref, g_ref, p_ref, st, fo, sg, own_slot, stage, slots):
     count = st.shape[0]
     R, _ = st.shape[-2:]
-    rows = s_hbm.shape[2]
-    fetch(((s_hbm.at[0], s_ref), (f_hbm.at[0], f_ref), (g_hbm.at[0], g_ref), (p_hbm, p_ref)), sems)
+    rows = s_ref.shape[1]
     for ch in range(2 * count + 1):
         kind, v = divmod(ch, count)
         x = g_ref[...] if kind == 2 else (s_ref, f_ref)[kind][v]
@@ -184,21 +178,24 @@
 def down_kernel(
     st, fo, sg, own_slot, below, above,
     u1, source, sigma, cells, head, tail, loop,
-    start, buf_a, buf_b, edge_buf, resid, own_loop,
+    start, buf_a, buf_b, edge_buf, box, resid, own_loop,
 ):
     count = st.shape[0]
     R, J = st.shape[-2:]
-    N = loop.shape[2]
     edge = FOLD
     row = lax.axis_index("row")
     blk = lax.axis_index("blk")
     blocks = lax.axis_size("blk")
+    slots = own_loop.shape[1]
+    N = blocks * slots
     sub = rows_of(R, J)
-    for ch in range(2 * count + 1):
-        x = jnp.concatenate(
-            [below[ch * edge : (ch + 1) * edge], above[ch * edge : (ch + 1) * edge]], axis=0
-        )
-        for b, part in enumerate(split_lanes(x)):
+    places, end = edge_rows(count)
+    for ch, (kind, v, at, width) in enumerate(places):
+        if width < edge:
+            box[...] = jnp.zeros_like(box)
+        box[edge - width : edge] = below[at : at + width]
+        box[edge : edge + width] = above[at : at + width]
+        for b, part in enumerate(split_lanes(box[...])):
             edge_buf[ch, b] = part
 
     def halo(ch, a, b):
@@ -207,11 +204,10 @@
         return jnp.where(sub == 0, high, jnp.where(sub == R - 1, low, 0.0))
 
     rows = R * FOLD
-    at = (2 * count + 1) * edge
     place = lanes_of(1, rows)
 
     def slot_of(message, i):
-        x = jnp.where(place == i, message[at : at + 1, :rows], 0.0)
+        x = jnp.where(place == i, message[end : end + 1, :rows], 0.0)
         return jnp.sum(x, axis=1, keepdims=True).astype(jnp.int32)
 
     for a in range(FOLD):
@@ -246,10 +242,14 @@
                 resid[v, a, b] = res[v]
                 u = src[v, a, b][:R]
                 u1[v, a, b] = u
-                at = (v * FOLD + a) * FOLD + b
+                at = (v * SECTIONS1 + a) * FOLD + b
                 k = (2 * count + 1) * 4 + at // R
-                head[k, at % R : at % R + 1] = u[:1]
-                tail[k, at % R : at % R + 1] = u[R - 1 :]
+                if a < SECTIONS1:
+                    head[k, at % R : at % R + 1] = u[:1]
+                at -= FOLD * (FOLD - SECTIONS1)
+                k = (2 * count + 1) * 4 + at // R
+                if a >= FOLD - SECTIONS1:
+                    tail[k, at % R : at % R + 1] = u[R - 1 :]
     for a in range(2):
         for b in range(2):
             for v in range(count):
@@ -267,19 +267,15 @@
             tail[at] = x
 
     lane = lanes_of(R, J)
-    ring = lanes_of(R, N)
-    sums = [jnp.zeros((R, N), jnp.float32) for _ in range(count)]
     column = jnp.where(row == 0, J - 1, 0)
+    sums = jnp.zeros((R, J), jnp.float32)
     for a in range(FOLD):
-        match = cells[a, :R, :1] == ring
+        slot = wrap(own_slot[a], slots)
         for v in range(count):
             face = jnp.where(row == 0, resid[v, a, FOLD - 1], resid[v, a, 0])
             face = jnp.sum(jnp.where(lane == column, face, 0.0), axis=1, keepdims=True)
-            sums[v] = sums[v] + jnp.where(match, face, 0.0)
-    own_loop[...] = jnp.zeros_like(own_loop)
-    for v in range(count):
-        own_loop[v : v + 1] = jnp.sum(sums[v], axis=0, keepdims=True)
-    loop[...] = jnp.broadcast_to(own_loop[...][None], loop.shape)
+            sums = sums + jnp.where(lane == slot + v * slots, face, 0.0)
+    loop[...] = jnp.broadcast_to(jnp.sum(sums, axis=0, keepdims=True), loop.shape)
 
 
 def up_kernel(
@@ -290,9 +286,10 @@
 ):
     count = u1.shape[0]
     R, J = u1.shape[-2:]
-    N = loop.shape[2]
+    N = corr_ref.shape[1]
     row = lax.axis_index("row")
     blk = lax.axis_index("blk")
+    blocks = lax.axis_size("blk")
     sub = rows_of(R, J)
     weights = pltpu.make_async_copy(weight_hbm, weight_ref, sem)
     weights.start()
@@ -360,19 +357,27 @@
         section(dst, src, n2, nf2, ns2, 0.25, 1.0 / (SECTIONS2 - k), 2, 2 * R)
         src = dst
 
-    half = loop.shape[0] // 2
-    rotor = jnp.sum(loop[:half], axis=0)
-    stator = jnp.sum(loop[half:], axis=0)
-    mine = jnp.where(row == 0, rotor, stator)
-    others = jnp.where(row == 0, stator, rotor)
+    slots = N // blocks
+    wide = loop.shape[1]
     offset = offset_ref[0]
+    shift = lax.rem(jnp.where(row == 0, N - offset, offset), N)
     weights.wait()
-    shift = lax.rem(jnp.where(row == 0, N - offset, offset), N)
+    both = []
+    for r in range(2):
+        held = loop[r * blocks : (r + 1) * blocks]
+        for v in range(count):
+            for c in range(0, N, wide):
+                cell = lanes_of(blocks, wide) + c
+                value = pick(held, cell // blocks + v * slots)
+                value = jnp.where(wrap(cell, blocks) == rows_of(blocks, wide), value, 0.0)
+                corr_ref[v : v + 1, c : c + wide] = jnp.sum(value, axis=0, keepdims=True)
+        both.append(corr_ref[...])
+    mine = jnp.where(row == 0, both[0], both[1])
+    others = jnp.where(row == 0, both[1], both[0])
     correction = weight_ref[...] * (mine + pltpu.roll(others, shift, 1))
     corr_ref[...] = correction
     length = loop_out.shape[2]
-    away = lax.rem(N - blk * length, N)
-    shown = pltpu.roll(correction, away, 1)
+    shown = pltpu.roll(correction, lax.rem(N - blk * length, N), 1)
     for v in range(count):
         loop_out[v] = shown[v : v + 1, :length]
 
@@ -382,12 +387,18 @@
                 after = src[v, a // 2, b // 2]
                 x = u2s[v, a // 2, b // 2]
                 gain = (after[:R] - x[:R], after[R:] - narrow(x)[1])
-                at = (v * FOLD + a) * FOLD + b
-                k = (2 * count + 1) * 4 + at // R
-                high = above[k, at % R : at % R + 1]
-                low = below[k, at % R : at % R + 1]
+                edges = gain[1]
+                for message, skip, half in (
+                    (above, 0, sub < R // 2),
+                    (below, FOLD - SECTIONS1, sub >= R // 2),
+                ):
+                    if skip <= a < skip + SECTIONS1:
+                        at = (v * SECTIONS1 + a - skip) * FOLD + b
+                        k = (2 * count + 1) * 4 + at // R
+                        x = message[k, at % R : at % R + 1]
+                        edges = edges + jnp.where(half, x, 0.0)
                 start[v, a, b, :R] = u1[v, a, b] + gain[0]
-                start[v, a, b, R:] = jnp.where(sub < R // 2, high, low) + gain[1]
+                start[v, a, b, R:] = edges
     lane = lanes_of(2 * R, J)
     ring = lanes_of(2 * R, N)
     last = jnp.logical_and(lane == J - 1, row == 0)
@@ -425,22 +436,22 @@
     held = lambda x: pltpu.with_memory_space_constraint(x, pltpu.VMEM)
     scratch = lambda *shape: pltpu.VMEM(shape, jnp.float32)
     far = pl.BlockSpec(memory_space=pltpu.HBM)
-    deep = 2 * FOLD
     slots = partner[:, :, 0]
-    packed = near(((2 * count + 2) * FOLD, cols))
+    packed = near((-(-(edge_rows(count)[1] + 1) // 8) * 8, cols))
     limit = pltpu.CompilerParams(vmem_limit_bytes=LIMIT)
-    head, tail = pl.pallas_call(
+    head, tail, s_near, f_near, g_near, p_near = pl.pallas_call(
         pack_kernel,
         in_specs=[far] * 4,
-        out_specs=[vmem()] * 2,
-        out_shape=[packed, packed],
-        scratch_shapes=[
-            scratch(2, count, deep, cols),
-            scratch(2, count, deep, cols),
-            scratch(2, deep, cols),
-            pltpu.VMEM((1, rows), jnp.int32),
-            pltpu.SemaphoreType.DMA((7,)),
+        out_specs=[vmem()] * 6,
+        out_shape=[
+            packed,
+            packed,
+            near((count, rows, cols)),
+            near((count, rows, cols)),
+            near((rows, cols)),
+            near((1, rows), jnp.int32),
         ],
+        scratch_shapes=[pltpu.SemaphoreType.DMA((4,))],
         compiler_params=limit,
         name="pack",
     )(away(state), away(forcing), away(sigma), away(slots))
@@ -451,7 +462,7 @@
 
     st, fo, sg, own_slot = pl.pallas_call(
         fold_kernel,
-        in_specs=[far] * 4,
+        in_specs=[vmem()] * 4,
         out_specs=[vmem()] * 4,
         out_shape=[
             near((count, FOLD, FOLD, R, J)),
@@ -460,20 +471,15 @@
             near((FOLD, R, J), jnp.int32),
         ],
         scratch_shapes=[
-            scratch(count, rows, cols),
-            scratch(count, rows, cols),
-            scratch(rows, cols),
-            pltpu.VMEM((1, rows), jnp.int32),
             scratch(2 * count + 1, FOLD, rows, J),
             pltpu.VMEM((rows, J), jnp.int32),
-            pltpu.SemaphoreType.DMA((4,)),
         ],
         compiler_params=limit,
         name="fold",
-    )(away(state), away(forcing), away(sigma), away(slots))
+    )(held(s_near), held(f_near), held(g_near), held(p_near))
 
     tiles = (2 * count + 1) * 4
-    message = near((tiles + count * FOLD * FOLD // R, R, J))
+    message = near((tiles - (-count * SECTIONS1 * FOLD // R), R, J))
     fine = (count, FOLD, FOLD, 2 * R, J)
     u1, source, sigma_w, cells, head, tail, loop = pl.pallas_call(
         down_kernel,
@@ -486,15 +492,16 @@
             near((FOLD, 2 * R, J), jnp.int32),
             message,
             message,
-            near((2 * blocks, 8, N)),
+            near((2 * blocks, J)),
         ],
         scratch_shapes=[
             scratch(*fine),
             scratch(*fine),
             scratch(*fine),
             scratch(2 * count + 1, FOLD, 2 * FOLD, J),
+            scratch(2 * FOLD, cols),
             scratch(count, FOLD, FOLD, R, J),
-            scratch(8, N),
+            scratch(8, length),
         ],
         compiler_params=limit,
         name="down",

time: 39.4 us -> 32.3 us (0.82)
  starting transfers between devices: 18.3 us -> 15.2 us
  waiting for transfers between devices: 10.8 us -> 7.89 us
  Pallas kernels: 8.66 us -> 7.65 us
    all_to_all x1, waiting for transfers between devices: 0.01 us -> 6.43 us  [body(): loop = lax.all_to_all(loop, ('row', 'blk'), 0, 0, tiled=True)]
    ppermute x2, waiting for transfers between devices: 6.48 us -> 1.45 us  [body(): below = lax.ppermute(tail, 'blk', up)]
    ppermute x2, waiting for transfers between devices: 4.32 us -> 0.01 us  [body(): above = lax.ppermute(head, 'blk', down)]
    all_to_all x1, starting transfers between devices: 5.74 us -> 2.54 us  [body(): loop = lax.all_to_all(loop, ('row', 'blk'), 0, 0, tiled=True)]
    pallas_call x2, Pallas kernels: 3.28 us -> 2.19 us  [the longest x1 1.17 us: body(): pl.pallas_call(pack_kernel, in_specs=[far] * 4, out_specs=[vmem()] * 6, o...]
    ppermute x2, starting transfers between devices: 3.02 us -> 3.63 us  [body(): below = lax.ppermute(tail, 'blk', up)]
    ppermute x2, starting transfers between devices: 9.58 us -> 9.07 us  [body(): above = lax.ppermute(head, 'blk', down)]
  transfers between devices with their start and end apart: 5 -> 5, of which waited for: 3 -> 2; matrix products, arithmetic and copies ran while one was open for 0% -> 0% of each run, Pallas kernels for 5% -> 3%
where the time goes in v2:
time: 32.3 us; the launch traced here: 32.1 us
  starting transfers between devices  15.2 us (47%)
  waiting for transfers between devices  7.89 us (24%)
  Pallas kernels  7.65 us (24%)
  between operations  1.3 us (4%)
    ppermute x2, starting transfers between devices, body(): above = lax.ppermute(head, 'blk', down)  9.07 us
    all_to_all x1, waiting for transfers between devices, body(): loop = lax.all_to_all(loop, ('row', 'blk'), 0, 0, tiled=True)  6.43 us
    ppermute x2, starting transfers between devices, body(): below = lax.ppermute(tail, 'blk', up)  3.63 us
    pallas_call x1, Pallas kernels, body(): pl.pallas_call(up_kernel, in_specs=[vmem()] * 8 + [far, pl.BlockSpec(memo...  3.37 us
    all_to_all x1, starting transfers between devices, body(): loop = lax.all_to_all(loop, ('row', 'blk'), 0, 0, tiled=True)  2.54 us
    pallas_call x1, Pallas kernels, body(): pl.pallas_call(down_kernel, in_specs=[vmem()] * 6, out_specs=[vmem()] * 7...  2.09 us
    ppermute x2, waiting for transfers between devices, body(): below = lax.ppermute(tail, 'blk', up)  1.45 us
    pallas_call x1, Pallas kernels, body(): pl.pallas_call(pack_kernel, in_specs=[far] * 4, out_specs=[vmem()] * 6, o...  1.17 us
  transfers between devices with their start and end apart: 5, of which 2 were waited for; matrix products, arithmetic and copies ran while one was open for 0% of the time, Pallas kernels for 3%

profile of v2, /device:TPU:0, one launch (start us, length us, event | category | flops | bytes accessed | tf_op | source)
XLA Modules:
  0.0 32.1 jit_solution(1840303324982527021)
XLA Ops:
  0.6 1.2 %pack.1 = (f32[40,512]{1,0:T(8,128)S(1)}, f32[40,512]{1,0:T(8,128)S(1)}, f32[5,32,512]{2,1,0:T(8,128)S(1)}, f32[5,32,512]{2,1,0:T(8,128)S(1)}, f32[32,512]{1,0:T(8,128)S(1)}, /*index=5*/s32[1,32]{1,0:T(1,128)S(1)}) custom-call(f32[1,5,32,512]{3,2,1,0:T(8,128)} %s_hbm.1, f32[1,5,32,512]{3,2,1,0:T(8,128)} %f_hbm.1, f32[1,32,512]{2,1,0:T(8,128)} %g_hbm.1, ...), custom_call_target="tpu_custom_call" | custom-call | tf_op jit(solution)/shard_map/pack/pallas_call | solution.py:442
  1.8 3.0 %collective-permute-start = (f32[40,512]{1,0:T(8,128)S(1)}, f32[40,512]{1,0:T(8,128)S(1)}, u32[]{:S(2)}, u32[]{:S(2)}) collective-permute-start(f32[40,512]{1,0:T(8,128)S(1)} %get-tuple-element.29), channel_id=1, source_target_pairs={{0,1},{1,2},{2,3},{3,4},{4,5},{5,6},{6,7},{7,8},{8,9},{9,10},{10,1... | collective-permute-start | bytes 245768 | tf_op jit(solution)/shard_map/ppermute | solution.py:460
  4.8 4.1 %collective-permute-start.1 = (f32[40,512]{1,0:T(8,128)S(1)}, f32[40,512]{1,0:T(8,128)S(1)}, u32[]{:S(2)}, u32[]{:S(2)}) collective-permute-start(f32[40,512]{1,0:T(8,128)S(1)} %get-tuple-element.30), channel_id=1, source_target_pairs={{1,0},{2,1},{3,2},{4,3},{5,4},{6,5},{7,6},{8,7},{9,8},{10,9},{11,1... | collective-permute-start | bytes 245768 | tf_op jit(solution)/shard_map/ppermute | solution.py:461
  8.9 1.0 %fold.1 = (f32[5,4,4,8,128]{4,3,2,1,0:T(8,128)S(1)}, f32[5,4,4,8,128]{4,3,2,1,0:T(8,128)S(1)}, f32[4,4,8,128]{3,2,1,0:T(8,128)S(1)}, s32[4,8,128]{2,1,0:T(8,128)S(1)}) custom-call(f32[5,32,512]{2,1,0:T(8,128)S(1)} %get-tuple-element.21.s_ref, f32[5,32,512]{2,1,0:T(8,128)S(1)} %get-tuple-element.22.f_ref, f32[32,512]{1,0:T(8,128)S(1)} %get-tuple-element.23.g_ref, ...), custom_call_target="tpu_custom_call" | custom-call | tf_op jit(solution)/shard_map/fold/pallas_call | solution.py:463
  9.9 1.5 %collective-permute-done.below = f32[40,512]{1,0:T(8,128)S(1)} collective-permute-done((f32[40,512]{1,0:T(8,128)S(1)}, f32[40,512]{1,0:T(8,128)S(1)}, u32[]{:S(2)}, u32[]{:S(2)}) %collective-permute-start) | collective-permute-done | bytes 81952 | tf_op jit(solution)/shard_map/ppermute | solution.py:460
  11.4 0.0 collective-permute-done.1.above
  11.4 2.1 %down.1 = (f32[5,4,4,8,128]{4,3,2,1,0:T(8,128)S(1)}, f32[5,4,4,16,128]{4,3,2,1,0:T(8,128)S(1)}, f32[4,4,16,128]{3,2,1,0:T(8,128)S(1)}, s32[4,16,128]{2,1,0:T(8,1...) custom-call(f32[5,4,4,8,128]{4,3,2,1,0:T(8,128)S(1)} %get-tuple-element.25.st, ...), custom_call_target="tpu_custom_call" | custom-call | tf_op jit(solution)/shard_map/down/pallas_call | solution.py:484
  13.5 0.6 %collective-permute-start.2 = (f32[52,8,128]{2,1,0:T(8,128)S(1)}, f32[52,8,128]{2,1,0:T(8,128)S(1)}, u32[]{:S(2)}, u32[]{:S(2)}) collective-permute-start(f32[52,8,128]{2,1,0:T(8,128)S(1)} %get-tuple-element.32), channel_id=1, source_target_pairs={{0,1},{1,2},{2,3},{3,4},{4,5},{5,6},{6,7},{7,8},{8,9},{9,10},{10,1... | collective-permute-start | bytes 638984 | tf_op jit(solution)/shard_map/ppermute | solution.py:510
  14.1 5.0 %collective-permute-start.3 = (f32[52,8,128]{2,1,0:T(8,128)S(1)}, f32[52,8,128]{2,1,0:T(8,128)S(1)}, u32[]{:S(2)}, u32[]{:S(2)}) collective-permute-start(f32[52,8,128]{2,1,0:T(8,128)S(1)} %get-tuple-element.31.own), channel_id=1, source_target_pairs={{1,0},{2,1},{3,2},{4,3},{5,4},{6,5},{7,6},{8,7},{9,8},{10,9},{11,1... | collective-permute-start | bytes 638984 | tf_op jit(solution)/shard_map/ppermute | solution.py:511
  19.1 2.5 %all-to-all-start = ((f32[32,1,128]{2,1,0:T(1,128)}), f32[32,1,128]{2,1,0:T(1,128)S(1)}, u32[]{:S(2)}, u32[]{:S(2)}) async-start(f32[32,1,128]{2,1,0:T(1,128)} %bitcast.2), calls=%async_computation | async-start | bytes 32768 | tf_op jit(solution)/shard_map/all_to_all | solution.py:512
  22.3 6.4 %all-to-all-done = f32[32,1,128]{2,1,0:T(1,128)S(1)} async-done(((f32[32,1,128]{2,1,0:T(1,128)}), f32[32,1,128]{2,1,0:T(1,128)S(1)}, u32[]{:S(2)}, u32[]{:S(2)}) %all-to-all-start) | async-done | bytes 16416 | tf_op jit(solution)/shard_map/all_to_all | solution.py:512
  28.7 0.0 collective-permute-done.2.below
  28.7 0.0 collective-permute-done.3.above
  28.7 3.4 %up.1 = (f32[1,5,32,512]{3,2,1,0:T(8,128)}, f32[5,1,8]{2,1,0:T(1,128)}) custom-call(f32[52,8,128]{2,1,0:T(8,128)S(1)} %get-tuple-element.31.own, f32[52,8,128]{2,1,0:T(8,128)S(1)} %collective-permute-done.2.below, f32[52,8,128]{2,1,0:T(8,128)S(1)} %collective-permute-done.3.above, f32[5,4,4,8,128]{4,3,2,1,0:T(8,128)S(1)} %get-tuple-element.33.u1, ...), custom_call_target="tpu_custom_call" | custom-call | tf_op jit(solution)/shard_map/up/pallas_call | solution.py:517
Async XLA Ops:
  1.8 9.6 %collective-permute-start = (f32[40,512]{1,0:T(8,128)S(1)}, f32[40,512]{1,0:T(8,128)S(1)}, u32[]{:S(2)}, u32[]{:S(2)}) collective-permute-start(f32[40,512]{1,0:T(8,128)S(1)} %get-tuple-element.29), channel_id=1, source_target_pairs={{0,1},{1,2},{2,3},{3,4},{4,5},{5,6},{6,7},{7,8},{8,9},{9,10},{10,1... | collective-permute-start | bytes 245768 | tf_op jit(solution)/shard_map/ppermute | solution.py:460
  4.8 6.5 %collective-permute-start.1 = (f32[40,512]{1,0:T(8,128)S(1)}, f32[40,512]{1,0:T(8,128)S(1)}, u32[]{:S(2)}, u32[]{:S(2)}) collective-permute-start(f32[40,512]{1,0:T(8,128)S(1)} %get-tuple-element.30), channel_id=1, source_target_pairs={{1,0},{2,1},{3,2},{4,3},{5,4},{6,5},{7,6},{8,7},{9,8},{10,9},{11,1... | collective-permute-start | bytes 245768 | tf_op jit(solution)/shard_map/ppermute | solution.py:461
  13.5 15.3 %collective-permute-start.2 = (f32[52,8,128]{2,1,0:T(8,128)S(1)}, f32[52,8,128]{2,1,0:T(8,128)S(1)}, u32[]{:S(2)}, u32[]{:S(2)}) collective-permute-start(f32[52,8,128]{2,1,0:T(8,128)S(1)} %get-tuple-element.32), channel_id=1, source_target_pairs={{0,1},{1,2},{2,3},{3,4},{4,5},{5,6},{6,7},{7,8},{8,9},{9,10},{10,1... | collective-permute-start | bytes 638984 | tf_op jit(solution)/shard_map/ppermute | solution.py:510
  14.1 14.7 %collective-permute-start.3 = (f32[52,8,128]{2,1,0:T(8,128)S(1)}, f32[52,8,128]{2,1,0:T(8,128)S(1)}, u32[]{:S(2)}, u32[]{:S(2)}) collective-permute-start(f32[52,8,128]{2,1,0:T(8,128)S(1)} %get-tuple-element.31.own), channel_id=1, source_target_pairs={{1,0},{2,1},{3,2},{4,3},{5,4},{6,5},{7,6},{8,7},{9,8},{10,9},{11,1... | collective-permute-start | bytes 638984 | tf_op jit(solution)/shard_map/ppermute | solution.py:511
  19.1 9.6 %all-to-all-start = ((f32[32,1,128]{2,1,0:T(1,128)}), f32[32,1,128]{2,1,0:T(1,128)S(1)}, u32[]{:S(2)}, u32[]{:S(2)}) async-start(f32[32,1,128]{2,1,0:T(1,128)} %bitcast.2), calls=%async_computation | async-start | bytes 32768 | tf_op jit(solution)/shard_map/all_to_all | solution.py:512

commit v3 on v2

--- a/solution.py
+++ b/solution.py
@@ -94,22 +94,78 @@
     return out
 
 
-def section(dst, src, start, source, sigma, scale, weight, fold, rows):
+def section(dst, src, start, source, sigma, tau, scale, weight, fold, rows):
     for a in range(fold):
         for b in range(fold):
             diag = 4.0 * scale + sigma[a, b][:rows]
-            step = weight * (COEFF / (diag + 1.5))
+            step = weight * tau[a, b][:rows]
             res = residual(src, source, diag, scale, a, b, fold, rows)
             for v, r in enumerate(res):
                 dst[v, a, b, :rows] = start[v, a, b][:rows] + step * r
 
 
-def first_section(dst, start, coarse, sigma, scale, weight, fold):
+def first_section(dst, start, coarse, tau, weight, fold):
     for a in range(fold):
         for b in range(fold):
-            step = weight * (COEFF / (4.0 * scale + sigma[a, b] + 1.5))
+            step = weight * tau[a, b]
             for v in range(dst.shape[0]):
                 dst[v, a, b] = start[v, a, b] + step * coarse[v, a, b]
+
+
+def step_size(sigma, scale):
+    return COEFF / (4.0 * scale + sigma + 1.5)
+
+
+def fine_residual(src, edge, source, diag, b, a=None):
+    count = src.shape[0]
+    R, J = src.shape[-2:]
+    sub, lane = rows_of(R, J), lanes_of(R, J)
+    top = FOLD - 1
+    at = (lambda v, i: edge[v, i]) if a is None else (lambda v, i: src[v, a, i])
+    u = [at(v, b) for v in range(count)]
+    q = u[0] * u[0]
+    for v in range(1, count):
+        q = q + u[v] * u[v]
+    q = q * (1.0 / count)
+    factor = diag + 0.5 * q / (1.0 + q)
+    out = []
+    for v in range(count):
+        if a is None:
+            up = jnp.where(sub == FOLD, src[v, top, b, R - 1 :], pltpu.roll(u[v], 1, 0))
+            down = jnp.where(sub == top, src[v, 0, b, :1], pltpu.roll(u[v], R - 1, 0))
+        else:
+            if a:
+                up = src[v, a - 1, b]
+            else:
+                up = jnp.where(sub == 0, edge[v, b, top : top + 1], pltpu.roll(src[v, top, b], 1, 0))
+            if a < top:
+                down = src[v, a + 1, b]
+            else:
+                below = edge[v, b, FOLD : FOLD + 1]
+                down = jnp.where(sub == R - 1, below, pltpu.roll(src[v, 0, b], R - 1, 0))
+        left = at(v, b - 1) if b else jnp.where(lane == 0, 0.0, pltpu.roll(at(v, top), 1, 1))
+        right = at(v, b + 1) if b < top else jnp.where(lane == J - 1, 0.0, pltpu.roll(at(v, 0), J - 1, 1))
+        near = (up + down) + (left + right)
+        out.append((source[v, b] if a is None else source[v, a, b]) + near - factor * u[v])
+    return out
+
+
+def fine_section(dst, dst_edge, src, edge, start, start_edge, source, source_edge, sigma, tau, weight):
+    for a in range(FOLD + 1):
+        if a == FOLD and dst_edge is None:
+            continue
+        for b in range(FOLD):
+            diag = 4.0 + sigma[a, b]
+            step = weight * tau[a, b]
+            if a == FOLD:
+                res = fine_residual(src, edge, source_edge, diag, b)
+            else:
+                res = fine_residual(src, edge, source, diag, b, a)
+            for v, r in enumerate(res):
+                if a == FOLD:
+                    dst_edge[v, b] = start_edge[v, b] + step * r
+                else:
+                    dst[v, a, b] = start[v, a, b] + step * r
 
 
 def quarter(x):
@@ -177,94 +233,84 @@
 
 def down_kernel(
     st, fo, sg, own_slot, below, above,
-    u1, source, sigma, cells, head, tail, loop,
-    start, buf_a, buf_b, edge_buf, box, resid, own_loop,
+    u1, edges, sigma, tau, cells, head, tail, loop,
+    buf_a, buf_b, edge_a, edge_b, box, resid, own_loop,
 ):
     count = st.shape[0]
     R, J = st.shape[-2:]
-    edge = FOLD
     row = lax.axis_index("row")
     blk = lax.axis_index("blk")
     blocks = lax.axis_size("blk")
     slots = own_loop.shape[1]
     N = blocks * slots
+    rows = R * FOLD
     sub = rows_of(R, J)
     places, end = edge_rows(count)
     for ch, (kind, v, at, width) in enumerate(places):
-        if width < edge:
+        if width < FOLD:
             box[...] = jnp.zeros_like(box)
-        box[edge - width : edge] = below[at : at + width]
-        box[edge : edge + width] = above[at : at + width]
+        box[FOLD - width : FOLD] = below[at : at + width]
+        box[FOLD : FOLD + width] = above[at : at + width]
         for b, part in enumerate(split_lanes(box[...])):
-            edge_buf[ch, b] = part
-
-    def halo(ch, a, b):
-        low = edge_buf[ch, b, a : a + 1]
-        high = edge_buf[ch, b, edge + a : edge + a + 1]
-        return jnp.where(sub == 0, high, jnp.where(sub == R - 1, low, 0.0))
-
-    rows = R * FOLD
+            edges[ch, b] = part
+    for b in range(FOLD):
+        for a in range(FOLD):
+            sigma[a, b] = sg[a, b]
+            tau[a, b] = step_size(sg[a, b], 1.0)
+        sigma[FOLD, b] = edges[2 * count, b]
+        tau[FOLD, b] = step_size(edges[2 * count, b], 1.0)
+
     place = lanes_of(1, rows)
-
-    def slot_of(message, i):
+    high = lax.rem(blk + 1, blocks)
+    low = lax.rem(blk + blocks - 1, blocks)
+    column = jnp.zeros((R, J), jnp.int32)
+    for k in range(2 * FOLD):
+        message, i = (below, rows - FOLD + k) if k < FOLD else (above, k - FOLD)
         x = jnp.where(place == i, message[end : end + 1, :rows], 0.0)
-        return jnp.sum(x, axis=1, keepdims=True).astype(jnp.int32)
-
+        x = jnp.sum(x, axis=1, keepdims=True).astype(jnp.int32)
+        column = jnp.where(sub == k, jnp.broadcast_to(x, (R, J)), column)
+    cells[FOLD] = wrap(column * blocks + jnp.where(sub < FOLD, low, high), N)
+    for a in range(FOLD):
+        cells[a] = wrap(own_slot[a] * blocks + blk, N)
+
+    start_edge = edges.at[:count]
+    source_edge = edges.at[count : 2 * count]
+    src, edge = st, start_edge
+    for k in range(SECTIONS1):
+        dst = u1 if k == SECTIONS1 - 1 else (buf_a, buf_b)[k % 2]
+        dst_edge = (edge_a, edge_b)[k % 2]
+        fine_section(
+            dst, dst_edge, src, edge, st, start_edge, fo, source_edge, sigma, tau, 1.0 / (SECTIONS1 - k)
+        )
+        src, edge = dst, dst_edge
+
+    first = (2 * count + 1) * 4 * R
     for a in range(FOLD):
         for b in range(FOLD):
-            for v in range(count):
-                start[v, a, b, :R] = st[v, a, b]
-                start[v, a, b, R:] = halo(v, a, b)
-                source[v, a, b, :R] = fo[v, a, b]
-                source[v, a, b, R:] = halo(count + v, a, b)
-            sigma[a, b, :R] = sg[a, b]
-            sigma[a, b, R:] = halo(2 * count, a, b)
-        own = own_slot[a]
-        low = jnp.broadcast_to(slot_of(below, rows - edge + a), (R, J))
-        high = jnp.broadcast_to(slot_of(above, a), (R, J))
-        cells[a, :R] = wrap(own * blocks + blk, N)
-        cells[a, R:] = jnp.where(
-            sub < R // 2,
-            wrap(high * blocks + lax.rem(blk + 1, blocks), N),
-            wrap(low * blocks + lax.rem(blk + blocks - 1, blocks), N),
-        )
-
-    src = start
-    for k in range(SECTIONS1):
-        dst = (buf_a, buf_b)[k % 2]
-        section(dst, src, start, source, sigma, 1.0, 1.0 / (SECTIONS1 - k), FOLD, 2 * R)
-        src = dst
-
-    for a in range(FOLD):
-        for b in range(FOLD):
-            res = residual(src, source, 4.0 + sigma[a, b][:R], 1.0, a, b, FOLD, R)
+            res = fine_residual(u1, edge, fo, 4.0 + sigma[a, b], b, a)
             for v in range(count):
                 resid[v, a, b] = res[v]
-                u = src[v, a, b][:R]
-                u1[v, a, b] = u
-                at = (v * SECTIONS1 + a) * FOLD + b
-                k = (2 * count + 1) * 4 + at // R
+                at = first + (v * FOLD + b) * SECTIONS1 + a
                 if a < SECTIONS1:
-                    head[k, at % R : at % R + 1] = u[:1]
-                at -= FOLD * (FOLD - SECTIONS1)
-                k = (2 * count + 1) * 4 + at // R
+                    head[at : at + 1] = u1[v, a, b, :1]
+                at -= FOLD - SECTIONS1
                 if a >= FOLD - SECTIONS1:
-                    tail[k, at % R : at % R + 1] = u[R - 1 :]
+                    tail[at : at + 1] = u1[v, a, b, R - 1 :]
     for a in range(2):
         for b in range(2):
             for v in range(count):
-                at = (v * 2 + a) * 2 + b
+                at = ((v * 2 + a) * 2 + b) * R
                 x = quarter(lambda i, j: u1[v, 2 * a + i, 2 * b + j])
-                head[at] = x
-                tail[at] = x
-                at += 4 * count
+                head[at : at + R] = x
+                tail[at : at + R] = x
+                at += 4 * count * R
                 x = quarter(lambda i, j: resid[v, 2 * a + i, 2 * b + j])
-                head[at] = x
-                tail[at] = x
-            at = 8 * count + a * 2 + b
+                head[at : at + R] = x
+                tail[at : at + R] = x
+            at = (8 * count + a * 2 + b) * R
             x = quarter(lambda i, j: sg[2 * a + i, 2 * b + j])
-            head[at] = x
-            tail[at] = x
+            head[at : at + R] = x
+            tail[at : at + R] = x
 
     lane = lanes_of(R, J)
     column = jnp.where(row == 0, J - 1, 0)
@@ -279,10 +325,11 @@
 
 
 def up_kernel(
-    own, below, above, u1, source, sigma, cells, loop, weight_hbm, offset_ref,
+    own, below, above, u1, source, edges, sigma, tau, cells, loop, weight_hbm, offset_ref,
     solution_ref, loop_out,
-    u2s, r2s, s2, f2, u3s, r3s, s3, f3, buf2a, buf2b, buf3a, buf3b,
-    n2, nf2, ns2, nu2s, nb2, start, buf_a, buf_b, corr_ref, stage, weight_ref, sem,
+    u2s, r2s, s2, t2, f2, u3s, r3s, s3, t3, f3, buf2a, buf2b, buf3a, buf3b,
+    n2, nf2, ns2, nt2, mid_a, mid_b, start, buf_a, buf_b, edge, edge_a, edge_b,
+    corr_ref, stage, weight_ref, sem,
 ):
     count = u1.shape[0]
     R, J = u1.shape[-2:]
@@ -303,19 +350,19 @@
         else:
             a, b = divmod(at - 8 * count, 2)
             dst = s2.at[a, b]
-        dst[:R] = own[at]
-        dst[R : 2 * R] = above[at]
-        dst[2 * R :] = below[at]
+        for part, message in enumerate((own, above, below)):
+            dst[part * R : (part + 1) * R] = message[at * R : (at + 1) * R]
 
     for a in range(2):
         for b in range(2):
+            t2[a, b] = step_size(s2[a, b], 0.25)
             res = residual(u2s, r2s, 1.0 + s2[a, b], 0.25, a, b, 2, 3 * R)
             for v in range(count):
                 f2[v, a, b] = 2.0 * r2s[v, a, b] - res[v]
-    first_section(buf2a, u2s, r2s, s2, 0.25, 1.0 / SECTIONS2, 2)
+    first_section(buf2a, u2s, r2s, t2, 1.0 / SECTIONS2, 2)
     src, dst = buf2a, buf2b
     for k in range(1, SECTIONS2):
-        section(dst, src, u2s, f2, s2, 0.25, 1.0 / (SECTIONS2 - k), 2, 3 * R)
+        section(dst, src, u2s, f2, s2, t2, 0.25, 1.0 / (SECTIONS2 - k), 2, 3 * R)
         src, dst = dst, src
     u2, r2 = src, dst
     for a in range(2):
@@ -327,14 +374,15 @@
         u3s[v, 0, 0] = quarter(lambda i, j: u2[v, i, j])
         r3s[v, 0, 0] = quarter(lambda i, j: r2[v, i, j])
     s3[0, 0] = quarter(lambda i, j: s2[i, j])
+    t3[0, 0] = step_size(s3[0, 0], 0.0625)
 
     res = residual(u3s, r3s, 0.25 + s3[0, 0], 0.0625, 0, 0, 1, 3 * R)
     for v in range(count):
         f3[v, 0, 0] = 2.0 * r3s[v, 0, 0] - res[v]
-    first_section(buf3a, u3s, r3s, s3, 0.0625, 1.0 / SECTIONS3, 1)
+    first_section(buf3a, u3s, r3s, t3, 1.0 / SECTIONS3, 1)
     src3, dst3 = buf3a, buf3b
     for k in range(1, SECTIONS3):
-        section(dst3, src3, u3s, f3, s3, 0.0625, 1.0 / (SECTIONS3 - k), 1, 3 * R)
+        section(dst3, src3, u3s, f3, s3, t3, 0.0625, 1.0 / (SECTIONS3 - k), 1, 3 * R)
         src3, dst3 = dst3, src3
 
     def narrow(x):
@@ -350,11 +398,11 @@
                     nf2[v, a, b, at] = narrow(f2[v, a, b])[part]
                     if v == 0:
                         ns2[a, b, at] = narrow(s2[a, b])[part]
+                        nt2[a, b, at] = narrow(t2[a, b])[part]
     src = n2
-    spare = nu2s
     for k in range(SECTIONS2):
-        dst = (nb2, spare)[k % 2]
-        section(dst, src, n2, nf2, ns2, 0.25, 1.0 / (SECTIONS2 - k), 2, 2 * R)
+        dst = (mid_a, mid_b)[k % 2]
+        section(dst, src, n2, nf2, ns2, nt2, 0.25, 1.0 / (SECTIONS2 - k), 2, 2 * R)
         src = dst
 
     slots = N // blocks
@@ -381,45 +429,55 @@
     for v in range(count):
         loop_out[v] = shown[v : v + 1, :length]
 
-    for v in range(count):
-        for a in range(FOLD):
-            for b in range(FOLD):
-                after = src[v, a // 2, b // 2]
-                x = u2s[v, a // 2, b // 2]
-                gain = (after[:R] - x[:R], after[R:] - narrow(x)[1])
-                edges = gain[1]
-                for message, skip, half in (
-                    (above, 0, sub < R // 2),
-                    (below, FOLD - SECTIONS1, sub >= R // 2),
-                ):
-                    if skip <= a < skip + SECTIONS1:
-                        at = (v * SECTIONS1 + a - skip) * FOLD + b
-                        k = (2 * count + 1) * 4 + at // R
-                        x = message[k, at % R : at % R + 1]
-                        edges = edges + jnp.where(half, x, 0.0)
-                start[v, a, b, :R] = u1[v, a, b] + gain[0]
-                start[v, a, b, R:] = edges
-    lane = lanes_of(2 * R, J)
-    ring = lanes_of(2 * R, N)
+    first = (2 * count + 1) * 4 * R
+    for v in range(count):
+        for b in range(2):
+            rim = {}
+            for a in range(2):
+                x, after = u2s[v, a, b], src[v, a, b]
+                gain = after[:R] - x[:R]
+                rim[0, a] = src[v, a, b, 2 * R - 1 :] - u2s[v, a, b, 3 * R - 1 :]
+                rim[1, a] = src[v, a, b, R : R + 1] - u2s[v, a, b, R : R + 1]
+                for i in range(2):
+                    for j in range(2):
+                        at = (v, 2 * a + i, 2 * b + j)
+                        start[at] = u1[at] + gain
+            lower = jnp.where(sub < FOLD // 2, rim[0, 0], rim[0, 1])
+            upper = jnp.where(sub < FOLD + FOLD // 2, rim[1, 0], rim[1, 1])
+            gain = jnp.where(sub < FOLD, lower, upper)
+            for j in range(2):
+                tile = edge.at[v, 2 * b + j]
+                tile[...] = jnp.zeros((R, J), jnp.float32)
+                at = first + (v * FOLD + 2 * b + j) * SECTIONS1
+                tile[FOLD - SECTIONS1 : FOLD] = below[at : at + SECTIONS1]
+                tile[FOLD : FOLD + SECTIONS1] = above[at : at + SECTIONS1]
+                tile[...] = tile[...] + gain
+    lane = lanes_of(R, J)
+    ring = lanes_of(R, N)
     last = jnp.logical_and(lane == J - 1, row == 0)
-    first = jnp.logical_and(lane == 0, row == 1)
-    for a in range(FOLD):
+    nearest = jnp.logical_and(lane == 0, row == 1)
+    for a in range(FOLD + 1):
         match = cells[a, :, :1] == ring
         for v in range(count):
             fix = jnp.where(match, corr_ref[v : v + 1], 0.0)
             fix = jnp.sum(fix, axis=1, keepdims=True)
-            start[v, a, FOLD - 1] = start[v, a, FOLD - 1] + jnp.where(last, fix, 0.0)
-            start[v, a, 0] = start[v, a, 0] + jnp.where(first, fix, 0.0)
-    src = start
+            tiles = edge.at[v] if a == FOLD else start.at[v, a]
+            tiles[FOLD - 1] = tiles[FOLD - 1] + jnp.where(last, fix, 0.0)
+            tiles[0] = tiles[0] + jnp.where(nearest, fix, 0.0)
+    source_edge = edges.at[count : 2 * count]
+    src, src_edge = start, edge
     for k in range(SECTIONS1):
         dst = (buf_a, buf_b)[k % 2]
-        rows = R if k == SECTIONS1 - 1 else 2 * R
-        section(dst, src, start, source, sigma, 1.0, 1.0 / (SECTIONS1 - k), FOLD, rows)
-        src = dst
+        dst_edge = None if k == SECTIONS1 - 1 else (edge_a, edge_b)[k % 2]
+        fine_section(
+            dst, dst_edge, src, src_edge, start, edge, source, source_edge, sigma, tau,
+            1.0 / (SECTIONS1 - k),
+        )
+        src, src_edge = dst, dst_edge
     for v in range(count):
         for a in range(FOLD):
             for b in range(FOLD):
-                stage[v, b, pl.ds(a, R, stride=FOLD), :] = src[v, a, b, :R]
+                stage[v, b, pl.ds(a, R, stride=FOLD), :] = src[v, a, b]
         for c, x in enumerate(join_lanes([stage[v, b] for b in range(FOLD)])):
             solution_ref[0, v, :, c * J : (c + 1) * J] = x
 
@@ -478,18 +536,20 @@
         name="fold",
     )(held(s_near), held(f_near), held(g_near), held(p_near))
 
-    tiles = (2 * count + 1) * 4
-    message = near((tiles - (-count * SECTIONS1 * FOLD // R), R, J))
-    fine = (count, FOLD, FOLD, 2 * R, J)
-    u1, source, sigma_w, cells, head, tail, loop = pl.pallas_call(
+    far_rows = (2 * count + 1) * 4 * R + count * SECTIONS1 * FOLD
+    message = near((-(-far_rows // 8) * 8, J))
+    fine = (count, FOLD, FOLD, R, J)
+    rim = (count, FOLD, R, J)
+    u1, edges, sigma_w, tau, cells, head, tail, loop = pl.pallas_call(
         down_kernel,
         in_specs=[vmem()] * 6,
-        out_specs=[vmem()] * 7,
+        out_specs=[vmem()] * 8,
         out_shape=[
-            near((count, FOLD, FOLD, R, J)),
             near(fine),
-            near((FOLD, FOLD, 2 * R, J)),
-            near((FOLD, 2 * R, J), jnp.int32),
+            near((2 * count + 1, FOLD, R, J)),
+            near((FOLD + 1, FOLD, R, J)),
+            near((FOLD + 1, FOLD, R, J)),
+            near((FOLD + 1, R, J), jnp.int32),
             message,
             message,
             near((2 * blocks, J)),
@@ -497,10 +557,10 @@
         scratch_shapes=[
             scratch(*fine),
             scratch(*fine),
+            scratch(*rim),
+            scratch(*rim),
+            scratch(2 * FOLD, cols),
             scratch(*fine),
-            scratch(2 * count + 1, FOLD, 2 * FOLD, J),
-            scratch(2 * FOLD, cols),
-            scratch(count, FOLD, FOLD, R, J),
             scratch(8, length),
         ],
         compiler_params=limit,
@@ -516,15 +576,17 @@
     thin = (count, 2, 2, 2 * R, J)
     result, loop_out = pl.pallas_call(
         up_kernel,
-        in_specs=[vmem()] * 8 + [far, pl.BlockSpec(memory_space=pltpu.SMEM)],
+        in_specs=[vmem()] * 10 + [far, pl.BlockSpec(memory_space=pltpu.SMEM)],
         out_specs=[vmem()] * 2,
         out_shape=[real(state.shape), real((count, 1, length))],
         scratch_shapes=[
-            scratch(*mid), scratch(*mid), scratch(*mid[1:]), scratch(*mid),
-            scratch(*low), scratch(*low), scratch(*low[1:]), scratch(*low),
+            scratch(*mid), scratch(*mid), scratch(*mid[1:]), scratch(*mid[1:]), scratch(*mid),
+            scratch(*low), scratch(*low), scratch(*low[1:]), scratch(*low[1:]), scratch(*low),
             scratch(*mid), scratch(*mid), scratch(*low), scratch(*low),
-            scratch(*thin), scratch(*thin), scratch(*thin[1:]), scratch(*thin), scratch(*thin),
+            scratch(*thin), scratch(*thin), scratch(*thin[1:]), scratch(*thin[1:]),
+            scratch(*thin), scratch(*thin),
             scratch(*fine), scratch(*fine), scratch(*fine),
+            scratch(*rim), scratch(*rim), scratch(*rim),
             scratch(8, N),
             scratch(count, FOLD, rows, J),
             scratch(1, N),
@@ -533,8 +595,8 @@
         compiler_params=limit,
         name="up",
     )(
-        held(head), held(below), held(above), held(u1), held(source), held(sigma_w), held(cells),
-        held(loop), away(loop_weight), offset,
+        held(head), held(below), held(above), held(u1), held(fo), held(edges), held(sigma_w),
+        held(tau), held(cells), held(loop), away(loop_weight), offset,
     )
     return result, jnp.transpose(loop_out, (1, 0, 2))
 

time: 32.3 us -> 31.8 us (0.985)
  Pallas kernels: 7.65 us -> 7.17 us
    pallas_call x2, Pallas kernels: 5.46 us -> 4.98 us  [the longest x1 3.16 us: body(): pl.pallas_call(up_kernel, in_specs=[vmem()] * 10 + [far, pl.BlockSpec(mem...]
where the time goes in v3:
time: 31.8 us; the launch traced here: 31.6 us
  starting transfers between devices  15.2 us (48%)
  waiting for transfers between devices  7.89 us (25%)
  Pallas kernels  7.17 us (23%)
  between operations  1.3 us (4%)
    ppermute x2, starting transfers between devices, body(): above = lax.ppermute(head, 'blk', down)  9.07 us
    all_to_all x1, waiting for transfers between devices, body(): loop = lax.all_to_all(loop, ('row', 'blk'), 0, 0, tiled=True)  6.43 us
    ppermute x2, starting transfers between devices, body(): below = lax.ppermute(tail, 'blk', up)  3.63 us
    pallas_call x1, Pallas kernels, body(): pl.pallas_call(up_kernel, in_specs=[vmem()] * 10 + [far, pl.BlockSpec(mem...  3.16 us
    all_to_all x1, starting transfers between devices, body(): loop = lax.all_to_all(loop, ('row', 'blk'), 0, 0, tiled=True)  2.54 us
    pallas_call x1, Pallas kernels, body(): pl.pallas_call(down_kernel, in_specs=[vmem()] * 6, out_specs=[vmem()] * 8...  1.82 us
    ppermute x2, waiting for transfers between devices, body(): below = lax.ppermute(tail, 'blk', up)  1.45 us
    pallas_call x1, Pallas kernels, body(): pl.pallas_call(pack_kernel, in_specs=[far] * 4, out_specs=[vmem()] * 6, o...  1.17 us
  transfers between devices with their start and end apart: 5, of which 2 were waited for; matrix products, arithmetic and copies ran while one was open for 0% of the time, Pallas kernels for 3%

profile of v3, /device:TPU:0, one launch (start us, length us, event | category | flops | bytes accessed | tf_op | source)
XLA Modules:
  0.0 31.6 jit_solution(1899559703615200827)
XLA Ops:
  0.6 1.2 %pack.1 = (f32[40,512]{1,0:T(8,128)S(1)}, f32[40,512]{1,0:T(8,128)S(1)}, f32[5,32,512]{2,1,0:T(8,128)S(1)}, f32[5,32,512]{2,1,0:T(8,128)S(1)}, f32[32,512]{1,0:T(8,128)S(1)}, /*index=5*/s32[1,32]{1,0:T(1,128)S(1)}) custom-call(f32[1,5,32,512]{3,2,1,0:T(8,128)} %s_hbm.1, f32[1,5,32,512]{3,2,1,0:T(8,128)} %f_hbm.1, f32[1,32,512]{2,1,0:T(8,128)} %g_hbm.1, ...), custom_call_target="tpu_custom_call" | custom-call | tf_op jit(solution)/shard_map/pack/pallas_call | solution.py:500
  1.8 3.0 %collective-permute-start = (f32[40,512]{1,0:T(8,128)S(1)}, f32[40,512]{1,0:T(8,128)S(1)}, u32[]{:S(2)}, u32[]{:S(2)}) collective-permute-start(f32[40,512]{1,0:T(8,128)S(1)} %get-tuple-element.30), channel_id=1, source_target_pairs={{0,1},{1,2},{2,3},{3,4},{4,5},{5,6},{6,7},{7,8},{8,9},{9,10},{10,1... | collective-permute-start | bytes 245768 | tf_op jit(solution)/shard_map/ppermute | solution.py:518
  4.8 4.1 %collective-permute-start.1 = (f32[40,512]{1,0:T(8,128)S(1)}, f32[40,512]{1,0:T(8,128)S(1)}, u32[]{:S(2)}, u32[]{:S(2)}) collective-permute-start(f32[40,512]{1,0:T(8,128)S(1)} %get-tuple-element.31), channel_id=1, source_target_pairs={{1,0},{2,1},{3,2},{4,3},{5,4},{6,5},{7,6},{8,7},{9,8},{10,9},{11,1... | collective-permute-start | bytes 245768 | tf_op jit(solution)/shard_map/ppermute | solution.py:519
  8.9 1.0 %fold.1 = (f32[5,4,4,8,128]{4,3,2,1,0:T(8,128)S(1)}, f32[5,4,4,8,128]{4,3,2,1,0:T(8,128)S(1)}, f32[4,4,8,128]{3,2,1,0:T(8,128)S(1)}, s32[4,8,128]{2,1,0:T(8,128)S(1)}) custom-call(f32[5,32,512]{2,1,0:T(8,128)S(1)} %get-tuple-element.22.s_ref, f32[5,32,512]{2,1,0:T(8,128)S(1)} %get-tuple-element.23.f_ref, f32[32,512]{1,0:T(8,128)S(1)} %get-tuple-element.24.g_ref, ...), custom_call_target="tpu_custom_call" | custom-call | tf_op jit(solution)/shard_map/fold/pallas_call | solution.py:521
  9.9 1.5 %collective-permute-done.below = f32[40,512]{1,0:T(8,128)S(1)} collective-permute-done((f32[40,512]{1,0:T(8,128)S(1)}, f32[40,512]{1,0:T(8,128)S(1)}, u32[]{:S(2)}, u32[]{:S(2)}) %collective-permute-start) | collective-permute-done | bytes 81952 | tf_op jit(solution)/shard_map/ppermute | solution.py:518
  11.4 0.0 collective-permute-done.1.above
  11.4 1.8 %down.1 = (f32[5,4,4,8,128]{4,3,2,1,0:T(8,128)S(1)}, f32[11,4,8,128]{3,2,1,0:T(8,128)S(1)}, f32[5,4,8,128]{3,2,1,0:T(8,128)S(1)}, f32[5,4,8,128]{3,2,1,0:T(8,128...) custom-call(f32[5,4,4,8,128]{4,3,2,1,0:T(8,128)S(1)} %get-tuple-element.2, ...), custom_call_target="tpu_custom_call" | custom-call | tf_op jit(solution)/shard_map/down/pallas_call | solution.py:543
  13.2 0.6 %collective-permute-start.2 = (f32[416,128]{1,0:T(8,128)S(1)}, f32[416,128]{1,0:T(8,128)S(1)}, u32[]{:S(2)}, u32[]{:S(2)}) collective-permute-start(f32[416,128]{1,0:T(8,128)S(1)} %get-tuple-element.33), channel_id=1, source_target_pairs={{0,1},{1,2},{2,3},{3,4},{4,5},{5,6},{6,7},{7,8},{8,9},{9,10},{10,1... | collective-permute-start | bytes 638984 | tf_op jit(solution)/shard_map/ppermute | solution.py:570
  13.8 5.0 %collective-permute-start.3 = (f32[416,128]{1,0:T(8,128)S(1)}, f32[416,128]{1,0:T(8,128)S(1)}, u32[]{:S(2)}, u32[]{:S(2)}) collective-permute-start(f32[416,128]{1,0:T(8,128)S(1)} %get-tuple-element.32.own), channel_id=1, source_target_pairs={{1,0},{2,1},{3,2},{4,3},{5,4},{6,5},{7,6},{8,7},{9,8},{10,9},{11,1... | collective-permute-start | bytes 638984 | tf_op jit(solution)/shard_map/ppermute | solution.py:571
  18.8 2.5 %all-to-all-start = ((f32[32,1,128]{2,1,0:T(1,128)}), f32[32,1,128]{2,1,0:T(1,128)S(1)}, u32[]{:S(2)}, u32[]{:S(2)}) async-start(f32[32,1,128]{2,1,0:T(1,128)} %bitcast.2), calls=%async_computation | async-start | bytes 32768 | tf_op jit(solution)/shard_map/all_to_all | solution.py:572
  22.0 6.4 %all-to-all-done = f32[32,1,128]{2,1,0:T(1,128)S(1)} async-done(((f32[32,1,128]{2,1,0:T(1,128)}), f32[32,1,128]{2,1,0:T(1,128)S(1)}, u32[]{:S(2)}, u32[]{:S(2)}) %all-to-all-start) | async-done | bytes 16416 | tf_op jit(solution)/shard_map/all_to_all | solution.py:572
  28.4 0.0 collective-permute-done.2.below
  28.4 0.0 collective-permute-done.3.above
  28.4 3.2 %up.1 = (f32[1,5,32,512]{3,2,1,0:T(8,128)}, f32[5,1,8]{2,1,0:T(1,128)}) custom-call(f32[416,128]{1,0:T(8,128)S(1)} %get-tuple-element.32.own, f32[416,128]{1,0:T(8,128)S(1)} %collective-permute-done.2.below, f32[416,128]{1,0:T(8,128)S(1)} %collective-permute-done.3.above, f32[5,4,4,8,128]{4,3,2,1,0:T(8,128)S(1)} %get-tuple-element.34.u1, ...), custom_call_target="tpu_custom_call" | custom-call | tf_op jit(solution)/shard_map/up/pallas_call | solution.py:577
Async XLA Ops:
  1.8 9.6 %collective-permute-start = (f32[40,512]{1,0:T(8,128)S(1)}, f32[40,512]{1,0:T(8,128)S(1)}, u32[]{:S(2)}, u32[]{:S(2)}) collective-permute-start(f32[40,512]{1,0:T(8,128)S(1)} %get-tuple-element.30), channel_id=1, source_target_pairs={{0,1},{1,2},{2,3},{3,4},{4,5},{5,6},{6,7},{7,8},{8,9},{9,10},{10,1... | collective-permute-start | bytes 245768 | tf_op jit(solution)/shard_map/ppermute | solution.py:518
  4.8 6.5 %collective-permute-start.1 = (f32[40,512]{1,0:T(8,128)S(1)}, f32[40,512]{1,0:T(8,128)S(1)}, u32[]{:S(2)}, u32[]{:S(2)}) collective-permute-start(f32[40,512]{1,0:T(8,128)S(1)} %get-tuple-element.31), channel_id=1, source_target_pairs={{1,0},{2,1},{3,2},{4,3},{5,4},{6,5},{7,6},{8,7},{9,8},{10,9},{11,1... | collective-permute-start | bytes 245768 | tf_op jit(solution)/shard_map/ppermute | solution.py:519
  13.2 15.3 %collective-permute-start.2 = (f32[416,128]{1,0:T(8,128)S(1)}, f32[416,128]{1,0:T(8,128)S(1)}, u32[]{:S(2)}, u32[]{:S(2)}) collective-permute-start(f32[416,128]{1,0:T(8,128)S(1)} %get-tuple-element.33), channel_id=1, source_target_pairs={{0,1},{1,2},{2,3},{3,4},{4,5},{5,6},{6,7},{7,8},{8,9},{9,10},{10,1... | collective-permute-start | bytes 638984 | tf_op jit(solution)/shard_map/ppermute | solution.py:570
  13.8 14.7 %collective-permute-start.3 = (f32[416,128]{1,0:T(8,128)S(1)}, f32[416,128]{1,0:T(8,128)S(1)}, u32[]{:S(2)}, u32[]{:S(2)}) collective-permute-start(f32[416,128]{1,0:T(8,128)S(1)} %get-tuple-element.32.own), channel_id=1, source_target_pairs={{1,0},{2,1},{3,2},{4,3},{5,4},{6,5},{7,6},{8,7},{9,8},{10,9},{11,1... | collective-permute-start | bytes 638984 | tf_op jit(solution)/shard_map/ppermute | solution.py:571
  18.8 9.6 %all-to-all-start = ((f32[32,1,128]{2,1,0:T(1,128)}), f32[32,1,128]{2,1,0:T(1,128)S(1)}, u32[]{:S(2)}, u32[]{:S(2)}) async-start(f32[32,1,128]{2,1,0:T(1,128)} %bitcast.2), calls=%async_computation | async-start | bytes 32768 | tf_op jit(solution)/shard_map/all_to_all | solution.py:572

commit v4 on v3

--- a/solution.py
+++ b/solution.py
@@ -150,11 +150,12 @@
     return out
 
 
-def fine_section(dst, dst_edge, src, edge, start, start_edge, source, source_edge, sigma, tau, weight):
+def fine_section(dst, dst_edge, src, edge, start, start_edge, source, source_edge, sigma, tau, weight,
+                 groups=range(FOLD)):
     for a in range(FOLD + 1):
         if a == FOLD and dst_edge is None:
             continue
-        for b in range(FOLD):
+        for b in groups:
             diag = 4.0 + sigma[a, b]
             step = weight * tau[a, b]
             if a == FOLD:
@@ -168,6 +169,15 @@
                     dst[v, a, b] = start[v, a, b] + step * r
 
 
+class Mixed:
+    def __init__(self, base, fresh, groups, axis):
+        self.base, self.fresh, self.groups, self.axis = base, fresh, groups, axis
+        self.shape = base.shape
+
+    def __getitem__(self, at):
+        return (self.fresh if at[self.axis] in self.groups else self.base)[at]
+
+
 def quarter(x):
     return 0.25 * ((x(0, 0) + x(0, 1)) + (x(1, 0) + x(1, 1)))
 
@@ -194,9 +204,17 @@
     return out, at
 
 
-def pack_kernel(s_hbm, f_hbm, g_hbm, p_hbm, head, tail, s_ref, f_ref, g_ref, p_ref, sems):
+def pack_kernel(
+    s_hbm, f_hbm, g_hbm, p_hbm, w_hbm, head, tail, s_ref, f_ref, g_ref, p_ref, w_ref, sems
+):
     count, rows = s_ref.shape[:2]
-    fetch(((p_hbm, p_ref), (s_hbm.at[0], s_ref), (f_hbm.at[0], f_ref), (g_hbm.at[0], g_ref)), sems)
+    fetch(
+        (
+            (p_hbm, p_ref), (w_hbm, w_ref), (s_hbm.at[0], s_ref), (f_hbm.at[0], f_ref),
+            (g_hbm.at[0], g_ref),
+        ),
+        sems,
+    )
     places, end = edge_rows(count)
     for kind, v, at, width in places:
         x = g_ref if kind == 2 else (s_ref, f_ref)[kind].at[v]
@@ -324,22 +342,15 @@
     loop[...] = jnp.broadcast_to(jnp.sum(sums, axis=0, keepdims=True), loop.shape)
 
 
-def up_kernel(
-    own, below, above, u1, source, edges, sigma, tau, cells, loop, weight_hbm, offset_ref,
-    solution_ref, loop_out,
+def coarse_kernel(
+    own, below, above, u1, source, edges, sigma, tau,
+    start, edge, one, one_edge, two, two_edge,
     u2s, r2s, s2, t2, f2, u3s, r3s, s3, t3, f3, buf2a, buf2b, buf3a, buf3b,
-    n2, nf2, ns2, nt2, mid_a, mid_b, start, buf_a, buf_b, edge, edge_a, edge_b,
-    corr_ref, stage, weight_ref, sem,
+    n2, nf2, ns2, nt2, mid_a, mid_b,
 ):
     count = u1.shape[0]
     R, J = u1.shape[-2:]
-    N = corr_ref.shape[1]
-    row = lax.axis_index("row")
-    blk = lax.axis_index("blk")
-    blocks = lax.axis_size("blk")
     sub = rows_of(R, J)
-    weights = pltpu.make_async_copy(weight_hbm, weight_ref, sem)
-    weights.start()
 
     for at in range(8 * count + 4):
         if at < 8 * count:
@@ -404,30 +415,6 @@
         dst = (mid_a, mid_b)[k % 2]
         section(dst, src, n2, nf2, ns2, nt2, 0.25, 1.0 / (SECTIONS2 - k), 2, 2 * R)
         src = dst
-
-    slots = N // blocks
-    wide = loop.shape[1]
-    offset = offset_ref[0]
-    shift = lax.rem(jnp.where(row == 0, N - offset, offset), N)
-    weights.wait()
-    both = []
-    for r in range(2):
-        held = loop[r * blocks : (r + 1) * blocks]
-        for v in range(count):
-            for c in range(0, N, wide):
-                cell = lanes_of(blocks, wide) + c
-                value = pick(held, cell // blocks + v * slots)
-                value = jnp.where(wrap(cell, blocks) == rows_of(blocks, wide), value, 0.0)
-                corr_ref[v : v + 1, c : c + wide] = jnp.sum(value, axis=0, keepdims=True)
-        both.append(corr_ref[...])
-    mine = jnp.where(row == 0, both[0], both[1])
-    others = jnp.where(row == 0, both[1], both[0])
-    correction = weight_ref[...] * (mine + pltpu.roll(others, shift, 1))
-    corr_ref[...] = correction
-    length = loop_out.shape[2]
-    shown = pltpu.roll(correction, lax.rem(N - blk * length, N), 1)
-    for v in range(count):
-        loop_out[v] = shown[v : v + 1, :length]
 
     first = (2 * count + 1) * 4 * R
     for v in range(count):
@@ -452,28 +439,85 @@
                 tile[FOLD - SECTIONS1 : FOLD] = below[at : at + SECTIONS1]
                 tile[FOLD : FOLD + SECTIONS1] = above[at : at + SECTIONS1]
                 tile[...] = tile[...] + gain
-    lane = lanes_of(R, J)
-    ring = lanes_of(R, N)
-    last = jnp.logical_and(lane == J - 1, row == 0)
-    nearest = jnp.logical_and(lane == 0, row == 1)
-    for a in range(FOLD + 1):
-        match = cells[a, :, :1] == ring
-        for v in range(count):
-            fix = jnp.where(match, corr_ref[v : v + 1], 0.0)
-            fix = jnp.sum(fix, axis=1, keepdims=True)
-            tiles = edge.at[v] if a == FOLD else start.at[v, a]
-            tiles[FOLD - 1] = tiles[FOLD - 1] + jnp.where(last, fix, 0.0)
-            tiles[0] = tiles[0] + jnp.where(nearest, fix, 0.0)
     source_edge = edges.at[count : 2 * count]
     src, src_edge = start, edge
-    for k in range(SECTIONS1):
-        dst = (buf_a, buf_b)[k % 2]
-        dst_edge = None if k == SECTIONS1 - 1 else (edge_a, edge_b)[k % 2]
+    for k, (dst, dst_edge) in enumerate(((one, one_edge), (two, two_edge))):
         fine_section(
             dst, dst_edge, src, src_edge, start, edge, source, source_edge, sigma, tau,
             1.0 / (SECTIONS1 - k),
         )
         src, src_edge = dst, dst_edge
+
+
+def fine_kernel(
+    start, edge, one, one_edge, two, two_edge, source, edges, sigma, tau, cells, loop, weight_ref,
+    offset_ref,
+    solution_ref, loop_out,
+    patch, patch_edge, buf_a, buf_b, edge_a, edge_b, corr_ref, stage,
+):
+    count = start.shape[0]
+    R, J = start.shape[-2:]
+    N = corr_ref.shape[1]
+    row = lax.axis_index("row")
+    blk = lax.axis_index("blk")
+    blocks = lax.axis_size("blk")
+    slots = N // blocks
+    wide = loop.shape[1]
+    offset = offset_ref[0]
+    shift = lax.rem(jnp.where(row == 0, N - offset, offset), N)
+    both = []
+    for r in range(2):
+        held = loop[r * blocks : (r + 1) * blocks]
+        for v in range(count):
+            for c in range(0, N, wide):
+                cell = lanes_of(blocks, wide) + c
+                value = pick(held, cell // blocks + v * slots)
+                value = jnp.where(wrap(cell, blocks) == rows_of(blocks, wide), value, 0.0)
+                corr_ref[v : v + 1, c : c + wide] = jnp.sum(value, axis=0, keepdims=True)
+        both.append(corr_ref[...])
+    mine = jnp.where(row == 0, both[0], both[1])
+    others = jnp.where(row == 0, both[1], both[0])
+    correction = weight_ref[...] * (mine + pltpu.roll(others, shift, 1))
+    corr_ref[...] = correction
+    length = loop_out.shape[2]
+    shown = pltpu.roll(correction, lax.rem(N - blk * length, N), 1)
+    for v in range(count):
+        loop_out[v] = shown[v : v + 1, :length]
+
+    lane = lanes_of(R, J)
+    ring = lanes_of(R, N)
+    source_edge = edges.at[count : 2 * count]
+
+    def smooth(side):
+        face, column = ((FOLD - 1, J - 1), (0, 0))[side]
+        for a in range(FOLD + 1):
+            match = cells[a, :, :1] == ring
+            for v in range(count):
+                fix = jnp.where(match, corr_ref[v : v + 1], 0.0)
+                fix = jnp.where(lane == column, jnp.sum(fix, axis=1, keepdims=True), 0.0)
+                if a == FOLD:
+                    patch_edge[v, face] = edge[v, face] + fix
+                else:
+                    patch[v, a, face] = start[v, a, face] + fix
+        first = Mixed(start, patch, (face,), 2)
+        first_edge = Mixed(edge, patch_edge, (face,), 1)
+        src, src_edge = first, first_edge
+        plain = ((one, one_edge), (two, two_edge), (None, None))
+        fresh = ((buf_a, edge_a), (buf_b, edge_b), (buf_a, None))
+        for k in range(SECTIONS1):
+            groups = [b for b in range(FOLD) if abs(b - face) <= k + 1 or k == SECTIONS1 - 1]
+            dst, dst_edge = fresh[k]
+            fine_section(
+                dst, dst_edge, src, src_edge, first, first_edge, source, source_edge, sigma, tau,
+                1.0 / (SECTIONS1 - k), groups,
+            )
+            if k < SECTIONS1 - 1:
+                src = Mixed(plain[k][0], dst, groups, 2)
+                src_edge = Mixed(plain[k][1], dst_edge, groups, 1)
+
+    for side in range(2):
+        pl.when(row == side)(functools.partial(smooth, side))
+    src = buf_a
     for v in range(count):
         for a in range(FOLD):
             for b in range(FOLD):
@@ -494,13 +538,14 @@
     held = lambda x: pltpu.with_memory_space_constraint(x, pltpu.VMEM)
     scratch = lambda *shape: pltpu.VMEM(shape, jnp.float32)
     far = pl.BlockSpec(memory_space=pltpu.HBM)
+    deep = 2 * FOLD
     slots = partner[:, :, 0]
     packed = near((-(-(edge_rows(count)[1] + 1) // 8) * 8, cols))
     limit = pltpu.CompilerParams(vmem_limit_bytes=LIMIT)
-    head, tail, s_near, f_near, g_near, p_near = pl.pallas_call(
+    head, tail, s_near, f_near, g_near, p_near, w_near = pl.pallas_call(
         pack_kernel,
-        in_specs=[far] * 4,
-        out_specs=[vmem()] * 6,
+        in_specs=[far] * 5,
+        out_specs=[vmem()] * 7,
         out_shape=[
             packed,
             packed,
@@ -508,11 +553,12 @@
             near((count, rows, cols)),
             near((rows, cols)),
             near((1, rows), jnp.int32),
+            near((1, N)),
         ],
-        scratch_shapes=[pltpu.SemaphoreType.DMA((4,))],
+        scratch_shapes=[pltpu.SemaphoreType.DMA((5,))],
         compiler_params=limit,
         name="pack",
-    )(away(state), away(forcing), away(sigma), away(slots))
+    )(away(state), away(forcing), away(sigma), away(slots), away(loop_weight))
     up = [(i, (i + 1) % blocks) for i in range(blocks)]
     down = [((i + 1) % blocks, i) for i in range(blocks)]
     below = lax.ppermute(tail, "blk", up)
@@ -574,29 +620,40 @@
     mid = (count, 2, 2, 3 * R, J)
     low = (count, 1, 1, 3 * R, J)
     thin = (count, 2, 2, 2 * R, J)
-    result, loop_out = pl.pallas_call(
-        up_kernel,
-        in_specs=[vmem()] * 10 + [far, pl.BlockSpec(memory_space=pltpu.SMEM)],
-        out_specs=[vmem()] * 2,
-        out_shape=[real(state.shape), real((count, 1, length))],
+    states = pl.pallas_call(
+        coarse_kernel,
+        in_specs=[vmem()] * 8,
+        out_specs=[vmem()] * 6,
+        out_shape=[near(fine), near(rim)] * 3,
         scratch_shapes=[
             scratch(*mid), scratch(*mid), scratch(*mid[1:]), scratch(*mid[1:]), scratch(*mid),
             scratch(*low), scratch(*low), scratch(*low[1:]), scratch(*low[1:]), scratch(*low),
             scratch(*mid), scratch(*mid), scratch(*low), scratch(*low),
             scratch(*thin), scratch(*thin), scratch(*thin[1:]), scratch(*thin[1:]),
             scratch(*thin), scratch(*thin),
-            scratch(*fine), scratch(*fine), scratch(*fine),
-            scratch(*rim), scratch(*rim), scratch(*rim),
+        ],
+        compiler_params=limit,
+        name="coarse",
+    )(
+        held(head), held(below), held(above), held(u1), held(fo), held(edges), held(sigma_w),
+        held(tau),
+    )
+    result, loop_out = pl.pallas_call(
+        fine_kernel,
+        in_specs=[vmem()] * 13 + [pl.BlockSpec(memory_space=pltpu.SMEM)],
+        out_specs=[vmem()] * 2,
+        out_shape=[real(state.shape), real((count, 1, length))],
+        scratch_shapes=[
+            scratch(*fine), scratch(*rim),
+            scratch(*fine), scratch(*fine), scratch(*rim), scratch(*rim),
             scratch(8, N),
             scratch(count, FOLD, rows, J),
-            scratch(1, N),
-            pltpu.SemaphoreType.DMA(()),
         ],
         compiler_params=limit,
-        name="up",
+        name="fine",
     )(
-        held(head), held(below), held(above), held(u1), held(fo), held(edges), held(sigma_w),
-        held(tau), held(cells), held(loop), away(loop_weight), offset,
+        *[held(x) for x in states], held(fo), held(edges), held(sigma_w), held(tau), held(cells),
+        held(loop), held(w_near), offset,
     )
     return result, jnp.transpose(loop_out, (1, 0, 2))
 

time: 31.8 us -> 30.7 us (0.965)
  waiting for transfers between devices: 7.89 us -> 6.29 us
  Pallas kernels: 7.17 us -> 7.63 us
    all_to_all x1, waiting for transfers between devices: 6.43 us -> 3.65 us  [body(): loop = lax.all_to_all(loop, ('row', 'blk'), 0, 0, tiled=True)]
    ppermute x2, waiting for transfers between devices: 1.45 us -> 2.64 us  [body(): below = lax.ppermute(tail, 'blk', up)]
    pallas_call x2 -> x3, Pallas kernels: 4.32 us -> 4.78 us  [the longest x1 2 us: body(): pl.pallas_call(fine_kernel, in_specs=[vmem()] * 13 + [pl.BlockSpec(memory...]
  transfers between devices with their start and end apart: 5 -> 5, of which waited for: 2 -> 3; matrix products, arithmetic and copies ran while one was open for 0% -> 0% of each run, Pallas kernels for 3% -> 9%
where the time goes in v4:
time: 30.7 us; the launch traced here: 30.5 us
  starting transfers between devices  15.2 us (50%)
  Pallas kernels  7.63 us (25%)
  waiting for transfers between devices  6.29 us (20%)
  between operations  1.31 us (4%)
    ppermute x2, starting transfers between devices, body(): above = lax.ppermute(head, 'blk', down)  9.07 us
    all_to_all x1, waiting for transfers between devices, body(): loop = lax.all_to_all(loop, ('row', 'blk'), 0, 0, tiled=True)  3.65 us
    ppermute x2, starting transfers between devices, body(): below = lax.ppermute(tail, 'blk', up)  3.63 us
    ppermute x2, waiting for transfers between devices, body(): below = lax.ppermute(tail, 'blk', up)  2.64 us
    all_to_all x1, starting transfers between devices, body(): loop = lax.all_to_all(loop, ('row', 'blk'), 0, 0, tiled=True)  2.54 us
    pallas_call x1, Pallas kernels, body(): pl.pallas_call(fine_kernel, in_specs=[vmem()] * 13 + [pl.BlockSpec(memory...  2 us
    pallas_call x1, Pallas kernels, body(): pl.pallas_call(down_kernel, in_specs=[vmem()] * 6, out_specs=[vmem()] * 8...  1.82 us
    pallas_call x1, Pallas kernels, body(): pl.pallas_call(coarse_kernel, in_specs=[vmem()] * 8, out_specs=[vmem()] *...  1.59 us
  transfers between devices with their start and end apart: 5, of which 3 were waited for; matrix products, arithmetic and copies ran while one was open for 0% of the time, Pallas kernels for 9%

profile of v4, /device:TPU:0, one launch (start us, length us, event | category | flops | bytes accessed | tf_op | source)
XLA Modules:
  0.0 30.5 jit_solution(5851316532843769951)
XLA Ops:
  0.6 1.2 %pack.1 = (f32[40,512]{1,0:T(8,128)S(1)}, f32[40,512]{1,0:T(8,128)S(1)}, f32[5,32,512]{2,1,0:T(8,128)S(1)}, f32[5,32,512]{2,1,0:T(8,128)S(1)}, f32[32,512]{1,0:T...) custom-call(f32[1,5,32,512]{3,2,1,0:T(8,128)} %s_hbm.1, f32[1,5,32,512]{3,2,1,0:T(8,128)} %f_hbm.1, ...), custom_call_target="tpu_custom_call" | custom-call | tf_op jit(solution)/shard_map/pack/pallas_call | solution.py:545
  1.8 3.0 %collective-permute-start = (f32[40,512]{1,0:T(8,128)S(1)}, f32[40,512]{1,0:T(8,128)S(1)}, u32[]{:S(2)}, u32[]{:S(2)}) collective-permute-start(f32[40,512]{1,0:T(8,128)S(1)} %get-tuple-element.37), channel_id=1, source_target_pairs={{0,1},{1,2},{2,3},{3,4},{4,5},{5,6},{6,7},{7,8},{8,9},{9,10},{10,1... | collective-permute-start | bytes 245768 | tf_op jit(solution)/shard_map/ppermute | solution.py:564
  4.8 4.1 %collective-permute-start.1 = (f32[40,512]{1,0:T(8,128)S(1)}, f32[40,512]{1,0:T(8,128)S(1)}, u32[]{:S(2)}, u32[]{:S(2)}) collective-permute-start(f32[40,512]{1,0:T(8,128)S(1)} %get-tuple-element.38), channel_id=1, source_target_pairs={{1,0},{2,1},{3,2},{4,3},{5,4},{6,5},{7,6},{8,7},{9,8},{10,9},{11,1... | collective-permute-start | bytes 245768 | tf_op jit(solution)/shard_map/ppermute | solution.py:565
  8.9 1.0 %fold.1 = (f32[5,4,4,8,128]{4,3,2,1,0:T(8,128)S(1)}, f32[5,4,4,8,128]{4,3,2,1,0:T(8,128)S(1)}, f32[4,4,8,128]{3,2,1,0:T(8,128)S(1)}, s32[4,8,128]{2,1,0:T(8,128)S(1)}) custom-call(f32[5,32,512]{2,1,0:T(8,128)S(1)} %get-tuple-element.29.s_ref, f32[5,32,512]{2,1,0:T(8,128)S(1)} %get-tuple-element.30.f_ref, f32[32,512]{1,0:T(8,128)S(1)} %get-tuple-element.31.g_ref, ...), custom_call_target="tpu_custom_call" | custom-call | tf_op jit(solution)/shard_map/fold/pallas_call | solution.py:567
  9.9 1.5 %collective-permute-done.below = f32[40,512]{1,0:T(8,128)S(1)} collective-permute-done((f32[40,512]{1,0:T(8,128)S(1)}, f32[40,512]{1,0:T(8,128)S(1)}, u32[]{:S(2)}, u32[]{:S(2)}) %collective-permute-start) | collective-permute-done | bytes 81952 | tf_op jit(solution)/shard_map/ppermute | solution.py:564
  11.4 0.0 collective-permute-done.1.above
  11.4 1.8 %down.1 = (f32[5,4,4,8,128]{4,3,2,1,0:T(8,128)S(1)}, f32[11,4,8,128]{3,2,1,0:T(8,128)S(1)}, f32[5,4,8,128]{3,2,1,0:T(8,128)S(1)}, f32[5,4,8,128]{3,2,1,0:T(8,128...) custom-call(f32[5,4,4,8,128]{4,3,2,1,0:T(8,128)S(1)} %get-tuple-element.3, ...), custom_call_target="tpu_custom_call" | custom-call | tf_op jit(solution)/shard_map/down/pallas_call | solution.py:589
  13.2 0.6 %collective-permute-start.2 = (f32[416,128]{1,0:T(8,128)S(1)}, f32[416,128]{1,0:T(8,128)S(1)}, u32[]{:S(2)}, u32[]{:S(2)}) collective-permute-start(f32[416,128]{1,0:T(8,128)S(1)} %get-tuple-element.40), channel_id=1, source_target_pairs={{0,1},{1,2},{2,3},{3,4},{4,5},{5,6},{6,7},{7,8},{8,9},{9,10},{10,1... | collective-permute-start | bytes 638984 | tf_op jit(solution)/shard_map/ppermute | solution.py:616
  13.8 5.0 %collective-permute-start.3 = (f32[416,128]{1,0:T(8,128)S(1)}, f32[416,128]{1,0:T(8,128)S(1)}, u32[]{:S(2)}, u32[]{:S(2)}) collective-permute-start(f32[416,128]{1,0:T(8,128)S(1)} %get-tuple-element.39.own), channel_id=1, source_target_pairs={{1,0},{2,1},{3,2},{4,3},{5,4},{6,5},{7,6},{8,7},{9,8},{10,9},{11,1... | collective-permute-start | bytes 638984 | tf_op jit(solution)/shard_map/ppermute | solution.py:617
  18.8 2.5 %all-to-all-start = ((f32[32,1,128]{2,1,0:T(1,128)}), f32[32,1,128]{2,1,0:T(1,128)S(1)}, u32[]{:S(2)}, u32[]{:S(2)}) async-start(f32[32,1,128]{2,1,0:T(1,128)} %bitcast.2), calls=%async_computation | async-start | bytes 32768 | tf_op jit(solution)/shard_map/all_to_all | solution.py:618
  22.0 1.2 %collective-permute-done.2.below = f32[416,128]{1,0:T(8,128)S(1)} collective-permute-done((f32[416,128]{1,0:T(8,128)S(1)}, f32[416,128]{1,0:T(8,128)S(1)}, u32[]{:S(2)}, u32[]{:S(2)}) %collective-permute-start.2) | collective-permute-done | bytes 213024 | tf_op jit(solution)/shard_map/ppermute | solution.py:616
  23.2 0.0 collective-permute-done.3.above
  23.2 1.6 %coarse.1 = (f32[5,4,4,8,128]{4,3,2,1,0:T(8,128)S(1)}, f32[5,4,8,128]{3,2,1,0:T(8,128)S(1)}, f32[5,4,4,8,128]{4,3,2,1,0:T(8,128)S(1)}, f32[5,4,8,128]{3,2,1,0:T(...) custom-call(f32[416,128]{1,0:T(8,128)S(1)} %get-tuple-element.39.own, ...), custom_call_target="tpu_custom_call" | custom-call | tf_op jit(solution)/shard_map/coarse/pallas_call | solution.py:623
  24.8 3.6 %all-to-all-done = f32[32,1,128]{2,1,0:T(1,128)S(1)} async-done(((f32[32,1,128]{2,1,0:T(1,128)}), f32[32,1,128]{2,1,0:T(1,128)S(1)}, u32[]{:S(2)}, u32[]{:S(2)}) %all-to-all-start) | async-done | bytes 16416 | tf_op jit(solution)/shard_map/all_to_all | solution.py:618
  28.5 2.0 %fine.1 = (f32[1,5,32,512]{3,2,1,0:T(8,128)}, f32[5,1,8]{2,1,0:T(1,128)}) custom-call(f32[5,4,4,8,128]{4,3,2,1,0:T(8,128)S(1)} %get-tuple-element.45.start, f32[5,4,8,128]{3,2,1,0:T(8,128)S(1)} %get-tuple-element.46.edge, f32[5,4,4,8,128]{4,3,2,1,0:T(8,128)S(1)} %get-tuple-element.47.one, f32[5,4,8,128]{3,2,1,0:T(8,128)S(1)} %get-tuple-element.48.one_edge, ...), custom_call_target="tpu_custom_call" | custom-call | tf_op jit(solution)/shard_map/fine/pallas_call | solution.py:641
Async XLA Ops:
  1.8 9.6 %collective-permute-start = (f32[40,512]{1,0:T(8,128)S(1)}, f32[40,512]{1,0:T(8,128)S(1)}, u32[]{:S(2)}, u32[]{:S(2)}) collective-permute-start(f32[40,512]{1,0:T(8,128)S(1)} %get-tuple-element.37), channel_id=1, source_target_pairs={{0,1},{1,2},{2,3},{3,4},{4,5},{5,6},{6,7},{7,8},{8,9},{9,10},{10,1... | collective-permute-start | bytes 245768 | tf_op jit(solution)/shard_map/ppermute | solution.py:564
  4.8 6.5 %collective-permute-start.1 = (f32[40,512]{1,0:T(8,128)S(1)}, f32[40,512]{1,0:T(8,128)S(1)}, u32[]{:S(2)}, u32[]{:S(2)}) collective-permute-start(f32[40,512]{1,0:T(8,128)S(1)} %get-tuple-element.38), channel_id=1, source_target_pairs={{1,0},{2,1},{3,2},{4,3},{5,4},{6,5},{7,6},{8,7},{9,8},{10,9},{11,1... | collective-permute-start | bytes 245768 | tf_op jit(solution)/shard_map/ppermute | solution.py:565
  13.2 10.0 %collective-permute-start.2 = (f32[416,128]{1,0:T(8,128)S(1)}, f32[416,128]{1,0:T(8,128)S(1)}, u32[]{:S(2)}, u32[]{:S(2)}) collective-permute-start(f32[416,128]{1,0:T(8,128)S(1)} %get-tuple-element.40), channel_id=1, source_target_pairs={{0,1},{1,2},{2,3},{3,4},{4,5},{5,6},{6,7},{7,8},{8,9},{9,10},{10,1... | collective-permute-start | bytes 638984 | tf_op jit(solution)/shard_map/ppermute | solution.py:616
  13.8 9.4 %collective-permute-start.3 = (f32[416,128]{1,0:T(8,128)S(1)}, f32[416,128]{1,0:T(8,128)S(1)}, u32[]{:S(2)}, u32[]{:S(2)}) collective-permute-start(f32[416,128]{1,0:T(8,128)S(1)} %get-tuple-element.39.own), channel_id=1, source_target_pairs={{1,0},{2,1},{3,2},{4,3},{5,4},{6,5},{7,6},{8,7},{9,8},{10,9},{11,1... | collective-permute-start | bytes 638984 | tf_op jit(solution)/shard_map/ppermute | solution.py:617
  18.8 9.6 %all-to-all-start = ((f32[32,1,128]{2,1,0:T(1,128)}), f32[32,1,128]{2,1,0:T(1,128)S(1)}, u32[]{:S(2)}, u32[]{:S(2)}) async-start(f32[32,1,128]{2,1,0:T(1,128)} %bitcast.2), calls=%async_computation | async-start | bytes 32768 | tf_op jit(solution)/shard_map/all_to_all | solution.py:618

commit v5 on v4

--- a/solution.py
+++ b/solution.py
@@ -51,13 +51,13 @@
     return out
 
 
-def join_lanes(parts):
+def join_lanes(parts, blocks=range(FOLD)):
     rows, wide = parts[0].shape
     run = wide // FOLD
     lane = lanes_of(rows, wide)
     turn = lane % FOLD
     out = []
-    for c in range(FOLD):
+    for c in blocks:
         index = lane // FOLD + c * run
         taken = [pick(p, index) for p in parts]
         value = taken[-1]
@@ -65,6 +65,14 @@
             value = jnp.where(turn == b, taken[b], value)
         out.append(value)
     return out
+
+
+def joined(tiles, stage, v, blocks=range(FOLD)):
+    R = tiles.shape[-2]
+    for a in range(FOLD):
+        for b in range(FOLD):
+            stage[v, b, pl.ds(a, R, stride=FOLD), :] = tiles[v, a, b]
+    return join_lanes([stage[v, b] for b in range(FOLD)], blocks)
 
 
 def residual(src, source, diag, scale, a, b, fold, rows):
@@ -344,9 +352,9 @@
 
 def coarse_kernel(
     own, below, above, u1, source, edges, sigma, tau,
-    start, edge, one, one_edge, two, two_edge,
+    start, edge, one, one_edge, two, two_edge, solution_hbm,
     u2s, r2s, s2, t2, f2, u3s, r3s, s3, t3, f3, buf2a, buf2b, buf3a, buf3b,
-    n2, nf2, ns2, nt2, mid_a, mid_b,
+    n2, nf2, ns2, nt2, mid_a, mid_b, three, stage, solution_ref, sems,
 ):
     count = u1.shape[0]
     R, J = u1.shape[-2:]
@@ -441,19 +449,28 @@
                 tile[...] = tile[...] + gain
     source_edge = edges.at[count : 2 * count]
     src, src_edge = start, edge
-    for k, (dst, dst_edge) in enumerate(((one, one_edge), (two, two_edge))):
+    for k, (dst, dst_edge) in enumerate(((one, one_edge), (two, two_edge), (three, None))):
         fine_section(
             dst, dst_edge, src, src_edge, start, edge, source, source_edge, sigma, tau,
             1.0 / (SECTIONS1 - k),
         )
         src, src_edge = dst, dst_edge
+    copies = []
+    for v in range(count):
+        for c, x in enumerate(joined(three, stage, v)):
+            solution_ref[v, :, c * J : (c + 1) * J] = x
+        copies.append(pltpu.make_async_copy(solution_ref.at[v], solution_hbm.at[0, v], sems.at[v]))
+        copies[-1].start()
+    for copy in copies:
+        copy.wait()
 
 
 def fine_kernel(
     start, edge, one, one_edge, two, two_edge, source, edges, sigma, tau, cells, loop, weight_ref,
-    offset_ref,
-    solution_ref, loop_out,
-    patch, patch_edge, buf_a, buf_b, edge_a, edge_b, corr_ref, stage,
+    offset_ref, old_hbm,
+    solution_hbm, loop_hbm,
+    patch, patch_edge, buf_a, buf_b, edge_a, edge_b, corr_ref, stage, strip, sem,
+    loop_out, loop_sem,
 ):
     count = start.shape[0]
     R, J = start.shape[-2:]
@@ -483,6 +500,8 @@
     shown = pltpu.roll(correction, lax.rem(N - blk * length, N), 1)
     for v in range(count):
         loop_out[v] = shown[v : v + 1, :length]
+    loop_copy = pltpu.make_async_copy(loop_out, loop_hbm, loop_sem)
+    loop_copy.start()
 
     lane = lanes_of(R, J)
     ring = lanes_of(R, N)
@@ -514,16 +533,16 @@
             if k < SECTIONS1 - 1:
                 src = Mixed(plain[k][0], dst, groups, 2)
                 src_edge = Mixed(plain[k][1], dst_edge, groups, 1)
+        c = face
+        for v in range(count):
+            (strip[v],) = joined(buf_a, stage, v, (c,))
+        copy = pltpu.make_async_copy(strip, solution_hbm.at[0, :, :, c * J : (c + 1) * J], sem)
+        copy.start()
+        copy.wait()
 
     for side in range(2):
         pl.when(row == side)(functools.partial(smooth, side))
-    src = buf_a
-    for v in range(count):
-        for a in range(FOLD):
-            for b in range(FOLD):
-                stage[v, b, pl.ds(a, R, stride=FOLD), :] = src[v, a, b]
-        for c, x in enumerate(join_lanes([stage[v, b] for b in range(FOLD)])):
-            solution_ref[0, v, :, c * J : (c + 1) * J] = x
+    loop_copy.wait()
 
 
 def body(state, forcing, sigma, partner, loop_weight, offset):
@@ -532,7 +551,6 @@
     N = loop_weight.shape[1]
     blocks = lax.axis_size("blk")
     length = N // blocks
-    real = functools.partial(jax.ShapeDtypeStruct, dtype=jnp.float32)
     near = lambda shape, dtype=jnp.float32: pltpu.VMEM(shape, dtype)
     away = lambda x: pltpu.with_memory_space_constraint(x, pltpu.HBM)
     held = lambda x: pltpu.with_memory_space_constraint(x, pltpu.VMEM)
@@ -620,17 +638,21 @@
     mid = (count, 2, 2, 3 * R, J)
     low = (count, 1, 1, 3 * R, J)
     thin = (count, 2, 2, 2 * R, J)
-    states = pl.pallas_call(
+    *states, result = pl.pallas_call(
         coarse_kernel,
         in_specs=[vmem()] * 8,
-        out_specs=[vmem()] * 6,
-        out_shape=[near(fine), near(rim)] * 3,
+        out_specs=[vmem()] * 6 + [far],
+        out_shape=[near(fine), near(rim)] * 3 + [pltpu.HBM(state.shape, jnp.float32)],
         scratch_shapes=[
             scratch(*mid), scratch(*mid), scratch(*mid[1:]), scratch(*mid[1:]), scratch(*mid),
             scratch(*low), scratch(*low), scratch(*low[1:]), scratch(*low[1:]), scratch(*low),
             scratch(*mid), scratch(*mid), scratch(*low), scratch(*low),
             scratch(*thin), scratch(*thin), scratch(*thin[1:]), scratch(*thin[1:]),
             scratch(*thin), scratch(*thin),
+            scratch(*fine),
+            scratch(count, FOLD, rows, J),
+            scratch(count, rows, cols),
+            pltpu.SemaphoreType.DMA((count,)),
         ],
         compiler_params=limit,
         name="coarse",
@@ -640,20 +662,25 @@
     )
     result, loop_out = pl.pallas_call(
         fine_kernel,
-        in_specs=[vmem()] * 13 + [pl.BlockSpec(memory_space=pltpu.SMEM)],
-        out_specs=[vmem()] * 2,
-        out_shape=[real(state.shape), real((count, 1, length))],
+        in_specs=[vmem()] * 13 + [pl.BlockSpec(memory_space=pltpu.SMEM), far],
+        out_specs=[far, far],
+        out_shape=[pltpu.HBM(state.shape, jnp.float32), pltpu.HBM((count, 1, length), jnp.float32)],
+        input_output_aliases={14: 0},
         scratch_shapes=[
             scratch(*fine), scratch(*rim),
             scratch(*fine), scratch(*fine), scratch(*rim), scratch(*rim),
             scratch(8, N),
             scratch(count, FOLD, rows, J),
+            scratch(count, rows, J),
+            pltpu.SemaphoreType.DMA(()),
+            scratch(count, 1, length),
+            pltpu.SemaphoreType.DMA(()),
         ],
         compiler_params=limit,
         name="fine",
     )(
         *[held(x) for x in states], held(fo), held(edges), held(sigma_w), held(tau), held(cells),
-        held(loop), held(w_near), offset,
+        held(loop), held(w_near), offset, result,
     )
     return result, jnp.transpose(loop_out, (1, 0, 2))
 

time: 30.7 us -> 30.3 us (0.987)
  waiting for transfers between devices: 6.29 us -> 5.09 us
  Pallas kernels: 7.63 us -> 8.52 us
    pallas_call x1, Pallas kernels: 1.59 us -> 2.84 us  [body(): pl.pallas_call(coarse_kernel, in_specs=[vmem()] * 8, out_specs=[vmem()] *...]
    all_to_all x1, waiting for transfers between devices: 3.65 us -> 2.41 us  [body(): loop = lax.all_to_all(loop, ('row', 'blk'), 0, 0, tiled=True)]
    pallas_call x1, Pallas kernels: 2 us -> 1.63 us  [body(): pl.pallas_call(fine_kernel, in_specs=[vmem()] * 13 + [pl.BlockSpec(memory...]
  transfers between devices with their start and end apart: 5 -> 5, of which waited for: 3 -> 3; matrix products, arithmetic and copies ran while one was open for 0% -> 0% of each run, Pallas kernels for 9% -> 13%
where the time goes in v5:
time: 30.3 us; the launch traced here: 30.1 us
  starting transfers between devices  15.2 us (50%)
  Pallas kernels  8.52 us (28%)
  waiting for transfers between devices  5.09 us (17%)
  between operations  1.31 us (4%)
    ppermute x2, starting transfers between devices, body(): above = lax.ppermute(head, 'blk', down)  9.07 us
    ppermute x2, starting transfers between devices, body(): below = lax.ppermute(tail, 'blk', up)  3.63 us
    pallas_call x1, Pallas kernels, body(): pl.pallas_call(coarse_kernel, in_specs=[vmem()] * 8, out_specs=[vmem()] *...  2.84 us
    ppermute x2, waiting for transfers between devices, body(): below = lax.ppermute(tail, 'blk', up)  2.67 us
    all_to_all x1, starting transfers between devices, body(): loop = lax.all_to_all(loop, ('row', 'blk'), 0, 0, tiled=True)  2.51 us
    all_to_all x1, waiting for transfers between devices, body(): loop = lax.all_to_all(loop, ('row', 'blk'), 0, 0, tiled=True)  2.41 us
    pallas_call x1, Pallas kernels, body(): pl.pallas_call(down_kernel, in_specs=[vmem()] * 6, out_specs=[vmem()] * 8...  1.82 us
    pallas_call x1, Pallas kernels, body(): pl.pallas_call(fine_kernel, in_specs=[vmem()] * 13 + [pl.BlockSpec(memory...  1.63 us
  transfers between devices with their start and end apart: 5, of which 3 were waited for; matrix products, arithmetic and copies ran while one was open for 0% of the time, Pallas kernels for 13%

profile of v5, /device:TPU:0, one launch (start us, length us, event | category | flops | bytes accessed | tf_op | source)
XLA Modules:
  0.0 30.1 jit_solution(8931122901313087219)
XLA Ops:
  0.6 1.2 %pack.1 = (f32[40,512]{1,0:T(8,128)S(1)}, f32[40,512]{1,0:T(8,128)S(1)}, f32[5,32,512]{2,1,0:T(8,128)S(1)}, f32[5,32,512]{2,1,0:T(8,128)S(1)}, f32[32,512]{1,0:T...) custom-call(f32[1,5,32,512]{3,2,1,0:T(8,128)} %s_hbm.1, f32[1,5,32,512]{3,2,1,0:T(8,128)} %f_hbm.1, ...), custom_call_target="tpu_custom_call" | custom-call | tf_op jit(solution)/shard_map/pack/pallas_call | solution.py:563
  1.8 3.0 %collective-permute-start = (f32[40,512]{1,0:T(8,128)S(1)}, f32[40,512]{1,0:T(8,128)S(1)}, u32[]{:S(2)}, u32[]{:S(2)}) collective-permute-start(f32[40,512]{1,0:T(8,128)S(1)} %get-tuple-element.38), channel_id=1, source_target_pairs={{0,1},{1,2},{2,3},{3,4},{4,5},{5,6},{6,7},{7,8},{8,9},{9,10},{10,1... | collective-permute-start | bytes 245768 | tf_op jit(solution)/shard_map/ppermute | solution.py:582
  4.8 4.1 %collective-permute-start.1 = (f32[40,512]{1,0:T(8,128)S(1)}, f32[40,512]{1,0:T(8,128)S(1)}, u32[]{:S(2)}, u32[]{:S(2)}) collective-permute-start(f32[40,512]{1,0:T(8,128)S(1)} %get-tuple-element.39), channel_id=1, source_target_pairs={{1,0},{2,1},{3,2},{4,3},{5,4},{6,5},{7,6},{8,7},{9,8},{10,9},{11,1... | collective-permute-start | bytes 245768 | tf_op jit(solution)/shard_map/ppermute | solution.py:583
  8.9 1.0 %fold.1 = (f32[5,4,4,8,128]{4,3,2,1,0:T(8,128)S(1)}, f32[5,4,4,8,128]{4,3,2,1,0:T(8,128)S(1)}, f32[4,4,8,128]{3,2,1,0:T(8,128)S(1)}, s32[4,8,128]{2,1,0:T(8,128)S(1)}) custom-call(f32[5,32,512]{2,1,0:T(8,128)S(1)} %get-tuple-element.30.s_ref, f32[5,32,512]{2,1,0:T(8,128)S(1)} %get-tuple-element.31.f_ref, f32[32,512]{1,0:T(8,128)S(1)} %get-tuple-element.32.g_ref, ...), custom_call_target="tpu_custom_call" | custom-call | tf_op jit(solution)/shard_map/fold/pallas_call | solution.py:585
  9.9 1.5 %collective-permute-done.below = f32[40,512]{1,0:T(8,128)S(1)} collective-permute-done((f32[40,512]{1,0:T(8,128)S(1)}, f32[40,512]{1,0:T(8,128)S(1)}, u32[]{:S(2)}, u32[]{:S(2)}) %collective-permute-start) | collective-permute-done | bytes 81952 | tf_op jit(solution)/shard_map/ppermute | solution.py:582
  11.4 0.0 collective-permute-done.1.above
  11.4 1.8 %down.1 = (f32[5,4,4,8,128]{4,3,2,1,0:T(8,128)S(1)}, f32[11,4,8,128]{3,2,1,0:T(8,128)S(1)}, f32[5,4,8,128]{3,2,1,0:T(8,128)S(1)}, f32[5,4,8,128]{3,2,1,0:T(8,128...) custom-call(f32[5,4,4,8,128]{4,3,2,1,0:T(8,128)S(1)} %get-tuple-element.3, ...), custom_call_target="tpu_custom_call" | custom-call | tf_op jit(solution)/shard_map/down/pallas_call | solution.py:607
  13.2 0.6 %collective-permute-start.2 = (f32[416,128]{1,0:T(8,128)S(1)}, f32[416,128]{1,0:T(8,128)S(1)}, u32[]{:S(2)}, u32[]{:S(2)}) collective-permute-start(f32[416,128]{1,0:T(8,128)S(1)} %get-tuple-element.41), channel_id=1, source_target_pairs={{0,1},{1,2},{2,3},{3,4},{4,5},{5,6},{6,7},{7,8},{8,9},{9,10},{10,1... | collective-permute-start | bytes 638984 | tf_op jit(solution)/shard_map/ppermute | solution.py:634
  13.8 5.0 %collective-permute-start.3 = (f32[416,128]{1,0:T(8,128)S(1)}, f32[416,128]{1,0:T(8,128)S(1)}, u32[]{:S(2)}, u32[]{:S(2)}) collective-permute-start(f32[416,128]{1,0:T(8,128)S(1)} %get-tuple-element.40.own), channel_id=1, source_target_pairs={{1,0},{2,1},{3,2},{4,3},{5,4},{6,5},{7,6},{8,7},{9,8},{10,9},{11,1... | collective-permute-start | bytes 638984 | tf_op jit(solution)/shard_map/ppermute | solution.py:635
  18.8 2.5 %all-to-all-start = ((f32[32,1,128]{2,1,0:T(1,128)}), f32[32,1,128]{2,1,0:T(1,128)S(1)}, u32[]{:S(2)}, u32[]{:S(2)}) async-start(f32[32,1,128]{2,1,0:T(1,128)} %bitcast.2), calls=%async_computation | async-start | bytes 32768 | tf_op jit(solution)/shard_map/all_to_all | solution.py:636
  22.0 1.2 %collective-permute-done.2.below = f32[416,128]{1,0:T(8,128)S(1)} collective-permute-done((f32[416,128]{1,0:T(8,128)S(1)}, f32[416,128]{1,0:T(8,128)S(1)}, u32[]{:S(2)}, u32[]{:S(2)}) %collective-permute-start.2) | collective-permute-done | bytes 213024 | tf_op jit(solution)/shard_map/ppermute | solution.py:634
  23.2 0.0 collective-permute-done.3.above
  23.2 2.8 %coarse.1 = (f32[5,4,4,8,128]{4,3,2,1,0:T(8,128)S(1)}, f32[5,4,8,128]{3,2,1,0:T(8,128)S(1)}, f32[5,4,4,8,128]{4,3,2,1,0:T(8,128)S(1)}, f32[5,4,8,128]{3,2,1,0:T(...) custom-call(f32[416,128]{1,0:T(8,128)S(1)} %get-tuple-element.40.own, ...), custom_call_target="tpu_custom_call" | custom-call | tf_op jit(solution)/shard_map/coarse/pallas_call | solution.py:641
  26.1 2.4 %all-to-all-done = f32[32,1,128]{2,1,0:T(1,128)S(1)} async-done(((f32[32,1,128]{2,1,0:T(1,128)}), f32[32,1,128]{2,1,0:T(1,128)S(1)}, u32[]{:S(2)}, u32[]{:S(2)}) %all-to-all-start) | async-done | bytes 16416 | tf_op jit(solution)/shard_map/all_to_all | solution.py:636
  28.5 1.6 %fine.1 = (f32[1,5,32,512]{3,2,1,0:T(8,128)}, f32[5,1,8]{2,1,0:T(1,128)}) custom-call(f32[5,4,4,8,128]{4,3,2,1,0:T(8,128)S(1)} %get-tuple-element.46.start, f32[5,4,8,128]{3,2,1,0:T(8,128)S(1)} %get-tuple-element.47.edge, f32[5,4,4,8,128]{4,3,2,1,0:T(8,128)S(1)} %get-tuple-element.48.one, ...), custom_call_target="tpu_custom_call", output_to_operand_aliasing={{0}: (14, {})} | custom-call | tf_op jit(solution)/shard_map/fine/pallas_call | solution.py:663
Async XLA Ops:
  1.8 9.6 %collective-permute-start = (f32[40,512]{1,0:T(8,128)S(1)}, f32[40,512]{1,0:T(8,128)S(1)}, u32[]{:S(2)}, u32[]{:S(2)}) collective-permute-start(f32[40,512]{1,0:T(8,128)S(1)} %get-tuple-element.38), channel_id=1, source_target_pairs={{0,1},{1,2},{2,3},{3,4},{4,5},{5,6},{6,7},{7,8},{8,9},{9,10},{10,1... | collective-permute-start | bytes 245768 | tf_op jit(solution)/shard_map/ppermute | solution.py:582
  4.8 6.5 %collective-permute-start.1 = (f32[40,512]{1,0:T(8,128)S(1)}, f32[40,512]{1,0:T(8,128)S(1)}, u32[]{:S(2)}, u32[]{:S(2)}) collective-permute-start(f32[40,512]{1,0:T(8,128)S(1)} %get-tuple-element.39), channel_id=1, source_target_pairs={{1,0},{2,1},{3,2},{4,3},{5,4},{6,5},{7,6},{8,7},{9,8},{10,9},{11,1... | collective-permute-start | bytes 245768 | tf_op jit(solution)/shard_map/ppermute | solution.py:583
  13.2 10.0 %collective-permute-start.2 = (f32[416,128]{1,0:T(8,128)S(1)}, f32[416,128]{1,0:T(8,128)S(1)}, u32[]{:S(2)}, u32[]{:S(2)}) collective-permute-start(f32[416,128]{1,0:T(8,128)S(1)} %get-tuple-element.41), channel_id=1, source_target_pairs={{0,1},{1,2},{2,3},{3,4},{4,5},{5,6},{6,7},{7,8},{8,9},{9,10},{10,1... | collective-permute-start | bytes 638984 | tf_op jit(solution)/shard_map/ppermute | solution.py:634
  13.8 9.4 %collective-permute-start.3 = (f32[416,128]{1,0:T(8,128)S(1)}, f32[416,128]{1,0:T(8,128)S(1)}, u32[]{:S(2)}, u32[]{:S(2)}) collective-permute-start(f32[416,128]{1,0:T(8,128)S(1)} %get-tuple-element.40.own), channel_id=1, source_target_pairs={{1,0},{2,1},{3,2},{4,3},{5,4},{6,5},{7,6},{8,7},{9,8},{10,9},{11,1... | collective-permute-start | bytes 638984 | tf_op jit(solution)/shard_map/ppermute | solution.py:635
  18.8 9.7 %all-to-all-start = ((f32[32,1,128]{2,1,0:T(1,128)}), f32[32,1,128]{2,1,0:T(1,128)S(1)}, u32[]{:S(2)}, u32[]{:S(2)}) async-start(f32[32,1,128]{2,1,0:T(1,128)} %bitcast.2), calls=%async_computation | async-start | bytes 32768 | tf_op jit(solution)/shard_map/all_to_all | solution.py:636
